TPU v7x, 32 devices: a whole 2x2x4 slice. The times are simulated.
32 devices in a mesh: row: 8 (over z, x), col: 4 (over y, core).
Axes of the slice: x: 2, y: 2, z: 4, core: 2. Of those that a mesh axis runs over, the one named last changes fastest.
Arguments:
- pixels: bfloat16 [512, 512, 384], P('row', 'col'), may hold values from -40 to 40, as said below
- start: float32 [384, 64], replicated, may hold values from -0.3125 to 0.3125
Outputs:
- mean: float32 [384], replicated
- projector: float32 [384, 384], replicated
- scores: float32 [64, 512, 512], P(None, 'row', 'col')
Inputs may be any that keep to these rules, and one draw needn't show every extreme that they name: `pixels`: Real-valued features.
All inputs are finite; a program needn't handle non-finite values.
Results may differ from a plain program's by a relative error of at most 0.0029.
Values may be sent and summed in bfloat16 or wider, within the bound.
No kernel may reach another device: no remote copies, remote signals or barrier semaphores. Data moves between devices by JAX's collectives and lax.ppermute only.
A program may use at most 64 MiB of HBM per device.

v0:
```python
import jax
import jax.numpy as jnp
from jax import lax
from jax.sharding import PartitionSpec as P

ITERS = 4


GAUSS = (0.0625, 0.25, 0.375, 0.25, 0.0625)


def padded_2(shard, sides, width):
    for axis, dim in sides:
        size, length = (lax.axis_size(axis), shard.shape[dim])
        up = [(i, (i + 1) % size) for i in range(size - 1)]
        down = [(j, i) for i, j in up]
        last = lax.slice_in_dim(shard, length - width, length, axis=dim)
        first = lax.slice_in_dim(shard, 0, width, axis=dim)
        before = lax.ppermute(last, axis, up)
        after = lax.ppermute(first, axis, down)
        shard = jnp.concatenate([before, shard, after], axis=dim)
    return shard


def edge_weight(first, count, total):
    position = first + jnp.arange(count, dtype=jnp.int32)
    weight = jnp.zeros((count,), jnp.float32)
    for offset in range(5):
        inside = (position + offset - 2 >= 0) & (position + offset - 2 < total)
        weight = weight + GAUSS[offset] * inside.astype(jnp.float32)
    return weight


def along_rows(padded, count):
    total = GAUSS[0] * padded[0:count].astype(jnp.float32)
    for offset in range(1, 5):
        total = total + GAUSS[offset] * padded[offset : offset + count].astype(jnp.float32)
    return total


def along_cols(padded, count):
    total = GAUSS[0] * padded[:, 0:count]
    for offset in range(1, 5):
        total = total + GAUSS[offset] * padded[:, offset : offset + count]
    return total


def orthonormal(product):
    inner = jnp.dot(product.T, product, precision=lax.Precision.HIGHEST)
    lower_factor = jnp.linalg.cholesky(inner)
    return lax.linalg.triangular_solve(
        lower_factor, product, left_side=False, lower=True, transpose_a=True
    )


def local(pixels, start):
    tile_rows, tile_cols, feat = pixels.shape
    rows_total = tile_rows * lax.axis_size("row")
    cols_total = tile_cols * lax.axis_size("col")
    padded = padded_2(pixels, (("row", 0), ("col", 1)), 2)
    blurred = along_cols(along_rows(padded, tile_rows), tile_cols)
    row_weight = edge_weight(lax.axis_index("row") * tile_rows, tile_rows, rows_total)
    col_weight = edge_weight(lax.axis_index("col") * tile_cols, tile_cols, cols_total)
    weight = row_weight[:, None, None] * col_weight[None, :, None]
    smoothed = (blurred / weight).astype(jnp.bfloat16)
    flat = smoothed.reshape(tile_rows * tile_cols, feat)
    gram_local = lax.dot_general(
        flat, flat, (((0,), (0,)), ((), ())), preferred_element_type=jnp.float32
    )
    sums_local = jnp.sum(flat, axis=0, dtype=jnp.float32)
    count = float(rows_total * cols_total)
    basis = start
    gram, sums = lax.psum((gram_local, sums_local), ("row", "col"))
    mean = sums / count
    cov = gram / count - mean[:, None] * mean[None, :]
    for step in range(ITERS):
        basis = orthonormal(jnp.dot(cov, basis, precision=lax.Precision.HIGHEST))
    projector = jnp.dot(basis, basis.T, precision=lax.Precision.HIGHEST)
    basis_b = basis.astype(jnp.bfloat16)
    shift = jnp.dot(mean, basis_b.astype(jnp.float32), precision=lax.Precision.HIGHEST)
    scores = lax.dot_general(
        basis_b, flat, (((0,), (1,)), ((), ())), preferred_element_type=jnp.float32
    )
    scores = scores - shift[:, None]
    return (mean, projector, scores.reshape(basis.shape[1], tile_rows, tile_cols))


def solution(mesh):
    in_specs = (P("row", "col", None), P())
    out_specs = (P(), P(), P(None, "row", "col"))
    return jax.shard_map(local, mesh=mesh, in_specs=in_specs, out_specs=out_specs, check_vma=False)
```

profile of v0, /device:TPU:0, one launch (start us, length us, event | category | flops | bytes accessed | tf_op | source)
XLA Modules:
  0.0 266.5 jit_solution(16941923063009096975)
XLA Ops:
  7.2 1.1 fusion.41
  8.3 4.9 %collective-permute-start = (bf16[2,128,384]{2,1,0:T(8,128)(2,1)S(1)}, bf16[2,128,384]{2,1,0:T(8,128)(2,1)S(1)}, u32[]{:S(2)}, u32[]{:S(2)}) collective-permute-start(bf16[2,128,384]{2,1,0:T(8,128)(2,1)S(1)} %get-tuple-element.10), channel_id=1, source_target_pairs={{0,4},{4,8},{8,12},{12,16},{16,20},{20,24},{24,28},{1,5},{5,9},{9,... | collective-permute-start | bytes 589832 | tf_op jit(solution)/shard_map/ppermute | solution.py:19
  13.2 1.3 collective-permute-start.1
  14.5 2.9 %collective-permute-done = bf16[2,128,384]{2,1,0:T(8,128)(2,1)S(1)} collective-permute-done((bf16[2,128,384]{2,1,0:T(8,128)(2,1)S(1)}, bf16[2,128,384]{2,1,0:T(8,128)(2,1)S(1)}, u32[]{:S(2)}, u32[]{:S(2)}) %collective-permute-start) | collective-permute-done | bytes 196640 | tf_op jit(solution)/shard_map/ppermute | solution.py:19
  17.4 4.6 %constant_dynamic-update-slice_fusion.1 = bf16[68,128,384]{2,1,0:T(8,128)(2,1)S(1)} fusion(bf16[68,128,384]{2,1,0:T(8,128)(2,1)S(1)} %constant_dynamic-update-slice_fusion.2, bf16[64,128,384]{2,1,0:T(8,128)(2,1)} %param.5), kind=kLoop, calls=%fused_computation.56 | loop fusion | bytes 12582912
  22.2 1.3 collective-permute-start.2
  23.5 1.3 collective-permute-start.3
  24.9 3.6 %collective-permute-done.3 = bf16[68,2,384]{2,1,0:T(2,128)(2,1)S(1)} collective-permute-done((bf16[68,2,384]{2,1,0:T(2,128)(2,1)S(1)}, bf16[68,2,384]{2,1,0:T(2,128)(2,1)S(1)}, u32[]{:S(2)}, u32[]{:S(2)}) %collective-permute-start.3) | collective-permute-done | bytes 104480 | tf_op jit(solution)/shard_map/ppermute | solution.py:20
  28.5 3.6 %pad_maximum_fusion = bf16[68,132,384]{2,1,0:T(8,128)(2,1)S(1)} fusion(bf16[68,2,384]{2,1,0:T(2,128)(2,1)S(1)} %collective-permute-done.3, bf16[68,128,384]{2,1,0:T(8,128)(2,1)S(1)} %constant_dynamic-update-slice_fusion, bf16[68,2,384]{2,1,0:T(2,128)(2,1)S(1)} %collective-permute-done.2), kind=kLoop, calls=%fused_computation.14 | loop fusion | flops 20680704 | bytes 13787136 | tf_op jit(solution)/shard_map/concatenate | solution.py:21
  32.1 6.2 %multiply_add_fusion = f32[64,132,384]{2,1,0:T(8,128)S(1)} fusion(bf16[68,132,384]{2,1,0:T(8,128)(2,1)S(1)} %pad_maximum_fusion), kind=kLoop, calls=%fused_computation | loop fusion | flops 45416448 | bytes 45416448 | tf_op jit(solution)/shard_map/add | solution.py:37
  38.3 9.7 %convert_reduce_fusion = (f32[384]{0:T(512)S(1)}, bf16[64,128,384]{2,1,0:T(8,128)(2,1)}) fusion(f32[64,128]{1,0:T(8,128)S(1)} %broadcast_multiply_fusion, f32[64,132,384]{2,1,0:T(8,128)S(1)} %multiply_add_fusion), kind=kLoop, calls=%fused_computation.11 | loop fusion | flops 40894080 | bytes 69240320 | tf_op jit(solution)/shard_map/reduce_sum | solution.py:70
  48.1 8.8 %convolution_bitcast_fusion = f32[384,384]{1,0:T(8,128)} fusion(bf16[64,128,384]{2,1,0:T(8,128)(2,1)} %get-tuple-element.6), kind=kOutput, calls=%fused_computation.16 | convolution fusion | flops 2415919104 | bytes 6881280 | tf_op jit(solution)/shard_map/dot_general | solution.py:67
  56.9 47.5 %psum.14 = f32[384]{0:T(512)S(1)} all-reduce(f32[384]{0:T(512)S(1)} %get-tuple-element.5), channel_id=1, replica_groups=mesh['row'=8,'col'=4] {'row','col'}, use_global_device_ids=true, to_apply=%region_1.0 | all-reduce | flops 384 | bytes 3072 | tf_op jit(solution)/shard_map/psum | solution.py:73
  104.5 88.2 %all-reduce.2.cloned.1.call-done = f32[384,384]{1,0:T(8,128)} async-done(((f32[384,384]{1,0:T(8,128)}), f32[384,384]{1,0:T(8,128)}) %all-reduce.2.cloned.1.call-update) | async-done | bytes 589840 | tf_op jit(solution)/shard_map/psum | solution.py:73
  192.7 1.9 fusion.38
  195.0 5.8 %cholesky.74 = f32[64,64]{1,0:T(8,128)S(1)} custom-call(f32[64,64]{1,0:T(8,128)S(1)} %fusion.18), custom_call_target="Cholesky" | custom-call | tf_op jit(solution)/shard_map/jit(cholesky)/cholesky | solution.py:50
  201.5 0.7 fusion.7
  202.2 4.9 %custom-call.8 = f32[1,64,64]{1,2,0:T(8,128)S(1)} custom-call(f32[1,64,64]{2,1,0:T(8,128)S(1)} %fusion.7), custom_call_target="InvertDiagBlocksLowerTriangular" | custom-call | tf_op jit(solution)/shard_map/triangular_solve/custom-call.0 | solution.py:51
  207.4 1.9 fusion.37
  209.7 5.8 %cholesky.85 = f32[64,64]{1,0:T(8,128)S(1)} custom-call(f32[64,64]{1,0:T(8,128)S(1)} %fusion.16), custom_call_target="Cholesky" | custom-call | tf_op jit(solution)/shard_map/jit(cholesky)/cholesky | solution.py:50
  216.2 0.7 fusion.8
  216.9 4.9 %custom-call.9 = f32[1,64,64]{1,2,0:T(8,128)S(1)} custom-call(f32[1,64,64]{2,1,0:T(8,128)S(1)} %fusion.8), custom_call_target="InvertDiagBlocksLowerTriangular" | custom-call | tf_op jit(solution)/shard_map/triangular_solve/custom-call.0 | solution.py:51
  222.1 1.9 fusion.36
  224.4 5.8 %cholesky.96 = f32[64,64]{1,0:T(8,128)S(1)} custom-call(f32[64,64]{1,0:T(8,128)S(1)} %fusion.14), custom_call_target="Cholesky" | custom-call | tf_op jit(solution)/shard_map/jit(cholesky)/cholesky | solution.py:50
  230.9 0.7 fusion.9
  231.6 4.9 %custom-call.10 = f32[1,64,64]{1,2,0:T(8,128)S(1)} custom-call(f32[1,64,64]{2,1,0:T(8,128)S(1)} %fusion.9), custom_call_target="InvertDiagBlocksLowerTriangular" | custom-call | tf_op jit(solution)/shard_map/triangular_solve/custom-call.0 | solution.py:51
  236.8 1.9 fusion.35
  239.1 5.8 %cholesky.107 = f32[64,64]{1,0:T(8,128)S(1)} custom-call(f32[64,64]{1,0:T(8,128)S(1)} %fusion.12), custom_call_target="Cholesky" | custom-call | tf_op jit(solution)/shard_map/jit(cholesky)/cholesky | solution.py:50
  246.2 4.9 %custom-call.11 = f32[1,64,64]{1,2,0:T(8,128)S(1)} custom-call(f32[1,64,64]{2,1,0:T(8,128)S(1)} %fusion.10), custom_call_target="InvertDiagBlocksLowerTriangular" | custom-call | tf_op jit(solution)/shard_map/triangular_solve/custom-call.0 | solution.py:51
  251.4 1.5 fusion.46
  253.0 4.9 %fusion.6 = f32[8,8,64,128]{3,1,2,0:T(8,128)S(1)} fusion(bf16[8192,384]{1,0:T(8,128)(2,1)} %bitcast.74, f32[64]{0:T(128)S(1)} %convolution_bitcast_fusion.5, f32[384,64]{0,1:T(8,128)S(1)} %convolution_bitcast_fusion.1), kind=kOutput, calls=%fused_computation.15 | convolution fusion | flops 403202048 | bytes 8487168 | tf_op jit(solution)/shard_map/dot_general | solution.py:81
  258.0 1.7 copy.11
  (42 shorter events, 6.4 us)
Async XLA Ops:
  7.2 185.6 %copy-start = (f32[384,64]{0,1:T(8,128)S(1)}, f32[384,64]{0,1:T(8,128)}, u32[]{:S(2)}) copy-start(f32[384,64]{0,1:T(8,128)} %param.6) | copy-start | bytes 294916
  7.2 185.6 %all-reduce.2.cloned.1.call-start = ((), (), s32[]{:S(2)}) async-start(), calls=%async_computation | async-start | bytes 1179648 | tf_op jit(solution)/shard_map/psum | solution.py:73
  8.3 9.1 %collective-permute-start = (bf16[2,128,384]{2,1,0:T(8,128)(2,1)S(1)}, bf16[2,128,384]{2,1,0:T(8,128)(2,1)S(1)}, u32[]{:S(2)}, u32[]{:S(2)}) collective-permute-start(bf16[2,128,384]{2,1,0:T(8,128)(2,1)S(1)} %get-tuple-element.10), channel_id=1, source_target_pairs={{0,4},{4,8},{8,12},{12,16},{16,20},{20,24},{24,28},{1,5},{5,9},{9,... | collective-permute-start | bytes 589832 | tf_op jit(solution)/shard_map/ppermute | solution.py:19
  13.2 8.8 %collective-permute-start.1 = (bf16[2,128,384]{2,1,0:T(8,128)(2,1)S(1)}, bf16[2,128,384]{2,1,0:T(8,128)(2,1)S(1)}, u32[]{:S(2)}, u32[]{:S(2)}) collective-permute-start(bf16[2,128,384]{2,1,0:T(8,128)(2,1)S(1)} %get-tuple-element.9), channel_id=1, source_target_pairs={{4,0},{8,4},{12,8},{16,12},{20,16},{24,20},{28,24},{5,1},{9,5},{13... | collective-permute-start | bytes 589832 | tf_op jit(solution)/shard_map/ppermute | solution.py:20
  22.2 2.7 %collective-permute-start.2 = (bf16[68,2,384]{2,1,0:T(2,128)(2,1)S(1)}, bf16[68,2,384]{2,1,0:T(2,128)(2,1)S(1)}, u32[]{:S(2)}, u32[]{:S(2)}) collective-permute-start(bf16[68,2,384]{2,1,0:T(2,128)(2,1)S(1)} %get-tuple-element.7), channel_id=1, source_target_pairs={{0,1},{1,2},{2,3},{4,5},{5,6},{6,7},{8,9},{9,10},{10,11},{12,13},{... | collective-permute-start | bytes 313352 | tf_op jit(solution)/shard_map/ppermute | solution.py:19
  23.5 5.0 %collective-permute-start.3 = (bf16[68,2,384]{2,1,0:T(2,128)(2,1)S(1)}, bf16[68,2,384]{2,1,0:T(2,128)(2,1)S(1)}, u32[]{:S(2)}, u32[]{:S(2)}) collective-permute-start(bf16[68,2,384]{2,1,0:T(2,128)(2,1)S(1)} %get-tuple-element.8), channel_id=1, source_target_pairs={{1,0},{2,1},{3,2},{5,4},{6,5},{7,6},{9,8},{10,9},{11,10},{13,12},{... | collective-permute-start | bytes 313352 | tf_op jit(solution)/shard_map/ppermute | solution.py:20
  104.5 155.2 %copy-start.1 = (f32[384]{0:T(512)}, f32[384]{0:T(512)S(1)}, u32[]{:S(2)}) copy-start(f32[384]{0:T(512)S(1)} %broadcast_multiply_fusion.1) | copy-start | bytes 4612
Sparse Core Ops, SparseCore 0:
  57.0 135.6 all-reduce.1
where the time goes:
time: 267 us
  waiting for transfers between devices  94.7 us (35%)
  other arithmetic  68 us (25%)
  blocking collectives  47.5 us (18%)
  matrix products  25.3 us (9%)
  between operations  14.4 us (5%)
  starting transfers between devices  8.8 us (3%)
  local copies, waits for them, and re-layouts  7.87 us (3%)
    psum x1, waiting for transfers between devices, local(): gram, sums = lax.psum((gram_local, sums_local), ('row', 'col'))  88.2 us
    psum x1, blocking collectives, local(): gram, sums = lax.psum((gram_local, sums_local), ('row', 'col'))  47.5 us
    another operation x12, other arithmetic, orthonormal(): lower_factor = jnp.linalg.cholesky(inner)  26.1 us
    another operation x8, other arithmetic, orthonormal(): lax.linalg.triangular_solve(lower_factor, product, left_side=False, lower...  22.2 us
    reduce_sum x1, other arithmetic, local(): sums_local = jnp.sum(flat, axis=0, dtype=jnp.float32)  9.75 us
    dot_general x1, matrix products, local(): lax.dot_general(flat, flat, (((0,), (0,)), ((), ())), preferred_element_t...  8.85 us
    dot_general x4, matrix products, local(): basis = orthonormal(jnp.dot(cov, basis, precision=lax.Precision.HIGHEST))  7.72 us
    unnamed x7, local copies, waits for them, and re-layouts  6.31 us
  transfers between devices with their start and end apart: 5, of which 3 were waited for; matrix products, arithmetic and copies ran while one was open for 2% of the time, Pallas kernels for 0%

commit v1 on v0

--- a/solution.py
+++ b/solution.py
@@ -1,10 +1,15 @@
+import functools
+
 import jax
 import jax.numpy as jnp
 from jax import lax
+from jax.experimental import pallas as pl
+from jax.experimental.pallas import tpu as pltpu
 from jax.sharding import PartitionSpec as P
 
 ITERS = 4
-
+LANES = 128
+HIGHEST = lax.Precision.HIGHEST
 
 GAUSS = (0.0625, 0.25, 0.375, 0.25, 0.0625)
 
@@ -45,12 +50,173 @@
     return total
 
 
-def orthonormal(product):
-    inner = jnp.dot(product.T, product, precision=lax.Precision.HIGHEST)
-    lower_factor = jnp.linalg.cholesky(inner)
-    return lax.linalg.triangular_solve(
-        lower_factor, product, left_side=False, lower=True, transpose_a=True
-    )
+def pack_gram(gram, sums):
+    n = gram.shape[0] // LANES
+    row = lax.broadcasted_iota(jnp.int32, (LANES, LANES), 0)
+    col = lax.broadcasted_iota(jnp.int32, (LANES, LANES), 1)
+    blocks = []
+    for i in range(n):
+        for j in range(i, n):
+            block = gram[i * LANES : (i + 1) * LANES, j * LANES : (j + 1) * LANES]
+            if i == j:
+                piece = sums[i * LANES : (i + 1) * LANES]
+                block = jnp.where((row == LANES - 1) & (col < LANES - 1), piece[None, :], block)
+                block = jnp.where((row == LANES - 2) & (col == 0), piece[LANES - 1], block)
+            blocks.append(block)
+    return jnp.concatenate(blocks, axis=0)
+
+
+def all_sum(values):
+    axes = ("row", "col")
+    rows, cols = lax.axis_size("row"), lax.axis_size("col")
+    if rows & (rows - 1) or cols & (cols - 1) or cols < 2:
+        return lax.psum(values, axes)
+
+    def pairs(row_bit, col_bit):
+        return [(r * cols + c, (r ^ row_bit) * cols + (c ^ col_bit)) for r in range(rows) for c in range(cols)]
+
+    core = pairs(0, 1)
+    odd = lax.axis_index("col") % 2
+    half = values.shape[0] // 2
+    mine = lax.dynamic_slice_in_dim(values, odd * half, half)
+    other = lax.dynamic_slice_in_dim(values, (1 - odd) * half, half)
+    kept = mine + lax.ppermute(other, axes, core)
+    row_steps = [pairs(1 << k, 0) for k in range(rows.bit_length() - 1)]
+    col_steps = [pairs(0, 1 << k) for k in range(1, cols.bit_length() - 1)]
+    order = row_steps[:1] + col_steps + row_steps[1:]
+    swapped = list(order)
+    for k in range(0, len(order) - 1, 2):
+        swapped[k], swapped[k + 1] = order[k + 1], order[k]
+    quarter = half // 2
+    a, b = kept[:quarter], kept[quarter:]
+    for first, second in zip(order, swapped):
+        got_a = lax.ppermute(a, axes, first)
+        got_b = lax.ppermute(b, axes, second)
+        a = a + got_a
+        b = b + got_b
+    kept = jnp.concatenate([a, b])
+    got = lax.ppermute(kept, axes, core)
+    return jnp.where(odd == 0, jnp.concatenate([kept, got]), jnp.concatenate([got, kept]))
+
+
+def inverse_factor(a):
+    n = a.shape[0]
+    row = lax.broadcasted_iota(jnp.int32, (n, n), 0)
+    col = lax.broadcasted_iota(jnp.int32, (n, n), 1)
+    work = jnp.concatenate([a, (row == col).astype(jnp.float32)], axis=1)
+    blocks = [work[8 * i : 8 * i + 8] for i in range(n // 8)]
+    sub = lax.broadcasted_iota(jnp.int32, (8, 2 * n), 0)
+    ahead = 4
+    pivots = []
+    for j0 in range(0, n, ahead):
+        first = j0 // 8
+        cols = [[jnp.broadcast_to(b[:, j0 + k : j0 + k + 1], (8, 2 * n)) for b in blocks[first:]] for k in range(ahead)]
+        for k in range(ahead):
+            j = j0 + k
+            s = j - 8 * first
+            recip = 1.0 / jnp.broadcast_to(cols[k][0][s : s + 1], (8, 2 * n))
+            pivots.append(recip)
+            line = jnp.broadcast_to(blocks[first][s : s + 1], (8, 2 * n)) * recip
+            factor = [c for c in cols[k]]
+            factor[0] = jnp.where(sub > s, factor[0], 0.0)
+            later = [jnp.broadcast_to(cols[m][0][s : s + 1], (8, 2 * n)) * recip for m in range(k + 1, ahead)]
+            for i in range(first, n // 8):
+                for m in range(k + 1, ahead):
+                    cols[m][i - first] = cols[m][i - first] - factor[i - first] * later[m - k - 1]
+                blocks[i] = blocks[i] - factor[i - first] * line
+    out = []
+    for i in range(n // 8):
+        scale = jnp.zeros((8, 2 * n), jnp.float32)
+        for s in range(8):
+            scale = jnp.where(sub == s, pivots[8 * i + s], scale)
+        out.append((blocks[i] * lax.rsqrt(1.0 / scale))[:, n:])
+    return jnp.concatenate(out, axis=0)
+
+
+def dot(a, b, contract, precision=HIGHEST):
+    return lax.dot_general(a, b, (contract, ((), ())), precision=precision, preferred_element_type=jnp.float32)
+
+
+def components_kernel(count, packed, start, smooth_hbm, mean_out, proj_out, scores_hbm, cov, smooth, scores, in_sem, out_sem):
+    feat = cov.shape[0]
+    n = feat // LANES
+    rank = start.shape[1]
+    tile_rows = smooth.shape[0]
+    fetch = pltpu.make_async_copy(smooth_hbm, smooth, in_sem)
+    fetch.start()
+    row = lax.broadcasted_iota(jnp.int32, (LANES, LANES), 0)
+    col = lax.broadcasted_iota(jnp.int32, (LANES, LANES), 1)
+    lane = lax.broadcasted_iota(jnp.int32, (1, LANES), 1)
+    inv = 1.0 / count
+    index = {}
+    for i in range(n):
+        for j in range(i, n):
+            index[i, j] = len(index)
+    block = lambda i, j: packed[index[i, j] * LANES : (index[i, j] + 1) * LANES, :]
+    means, mean_cols, diag = [], [], []
+    for i in range(n):
+        b = block(i, i)
+        bt = b.T
+        last = b[LANES - 2 : LANES - 1, 0:1]
+        m = jnp.where(lane < LANES - 1, b[LANES - 1 : LANES, :], last) * inv
+        means.append(m)
+        mean_cols.append(jnp.broadcast_to(m, (LANES, LANES)).T)
+        diag.append(jnp.where(row <= col, b, bt))
+    mean = jnp.concatenate(means, axis=1)
+    mean_out[...] = mean
+    for i in range(n):
+        for j in range(i, n):
+            g = diag[i] if i == j else block(i, j)
+            c = g * inv - mean_cols[i] * means[j]
+            cov[i * LANES : (i + 1) * LANES, j * LANES : (j + 1) * LANES] = c
+            if i != j:
+                cov[j * LANES : (j + 1) * LANES, i * LANES : (i + 1) * LANES] = c.T
+    basis = start[...].T
+    for step in range(ITERS):
+        y = dot(basis, cov[...], ((1,), (0,)))
+        lower = inverse_factor(dot(y, y, ((1,), (1,))))
+        basis = dot(lower, y, ((1,), (0,)))
+    proj_out[...] = dot(basis, basis, ((0,), (0,)))
+    basis_b = basis.astype(jnp.bfloat16)
+    shift = jnp.sum(basis_b.astype(jnp.float32) * mean, axis=1, keepdims=True)
+    shift = jnp.broadcast_to(shift, (rank, LANES))
+    fetch.wait()
+    for g in range(tile_rows // 8):
+        for h in range(8 * g, 8 * g + 8):
+            s = lax.dot_general(
+                basis_b, smooth[h], (((1,), (1,)), ((), ())), preferred_element_type=jnp.float32
+            )
+            scores[:, h, :] = s - shift
+        pltpu.make_async_copy(scores.at[:, pl.ds(8 * g, 8), :], scores_hbm.at[:, pl.ds(8 * g, 8), :], out_sem.at[g]).start()
+    for g in range(tile_rows // 8):
+        pltpu.make_async_copy(scores.at[:, pl.ds(8 * g, 8), :], scores_hbm.at[:, pl.ds(8 * g, 8), :], out_sem.at[g]).wait()
+
+
+def components(packed, start, smoothed, count):
+    tile_rows, tile_cols, feat = smoothed.shape
+    rank = start.shape[1]
+    vmem = pl.BlockSpec(memory_space=pltpu.VMEM)
+    hbm = pl.BlockSpec(memory_space=pl.ANY)
+    return pl.pallas_call(
+        functools.partial(components_kernel, count),
+        out_shape=(
+            jax.ShapeDtypeStruct((1, feat), jnp.float32),
+            jax.ShapeDtypeStruct((feat, feat), jnp.float32),
+            jax.ShapeDtypeStruct((rank, tile_rows, tile_cols), jnp.float32),
+        ),
+        in_specs=[vmem, vmem, hbm],
+        out_specs=(vmem, vmem, hbm),
+        scratch_shapes=[
+            pltpu.VMEM((feat, feat), jnp.float32),
+            pltpu.VMEM((tile_rows, tile_cols, feat), jnp.bfloat16),
+            pltpu.VMEM((rank, tile_rows, tile_cols), jnp.float32),
+            pltpu.SemaphoreType.DMA,
+            pltpu.SemaphoreType.DMA((tile_rows // 8,)),
+        ],
+        compiler_params=pltpu.CompilerParams(vmem_limit_bytes=32 << 20),
+        cost_estimate=pl.CostEstimate(flops=10**9, bytes_accessed=10**7, transcendentals=0),
+        name="components",
+    )(packed, start, smoothed)
 
 
 def local(pixels, start):
@@ -68,21 +234,9 @@
         flat, flat, (((0,), (0,)), ((), ())), preferred_element_type=jnp.float32
     )
     sums_local = jnp.sum(flat, axis=0, dtype=jnp.float32)
-    count = float(rows_total * cols_total)
-    basis = start
-    gram, sums = lax.psum((gram_local, sums_local), ("row", "col"))
-    mean = sums / count
-    cov = gram / count - mean[:, None] * mean[None, :]
-    for step in range(ITERS):
-        basis = orthonormal(jnp.dot(cov, basis, precision=lax.Precision.HIGHEST))
-    projector = jnp.dot(basis, basis.T, precision=lax.Precision.HIGHEST)
-    basis_b = basis.astype(jnp.bfloat16)
-    shift = jnp.dot(mean, basis_b.astype(jnp.float32), precision=lax.Precision.HIGHEST)
-    scores = lax.dot_general(
-        basis_b, flat, (((0,), (1,)), ((), ())), preferred_element_type=jnp.float32
-    )
-    scores = scores - shift[:, None]
-    return (mean, projector, scores.reshape(basis.shape[1], tile_rows, tile_cols))
+    packed = all_sum(pack_gram(gram_local, sums_local))
+    mean, projector, scores = components(packed, start, smoothed, float(rows_total * cols_total))
+    return (mean.reshape(feat), projector, scores)
 
 
 def solution(mesh):

time: 267 us -> 133 us (0.50)
  waiting for transfers between devices: 94.7 us -> 25 us
  blocking collectives: 47.5 us -> 0 us
  other arithmetic: 68 us -> 42.6 us
  Pallas kernels: 0 us -> 22 us
  matrix products: 25.3 us -> 3.42 us
  starting transfers between devices: 8.8 us -> 26.1 us
  between operations: 14.4 us -> 0.96 us
  local copies, waits for them, and re-layouts: 7.87 us -> 12.1 us
    psum x1 -> x0, waiting for transfers between devices: 88.2 us -> none  [local(): gram, sums = lax.psum((gram_local, sums_local), ('row', 'col'))]
    another operation x20 -> x0, other arithmetic: 48.3 us -> none  [the longest x12 26.1 us: orthonormal(): lower_factor = jnp.linalg.cholesky(inner)]
    psum x1 -> x0, blocking collectives: 47.5 us -> none  [local(): gram, sums = lax.psum((gram_local, sums_local), ('row', 'col'))]
    pallas_call x0 -> x1, Pallas kernels: none -> 22 us  [components(): pl.pallas_call(functools.partial(components_kernel, count), out_shape=(ja...]
    ppermute x0 -> x10, waiting for transfers between devices: none -> 18.6 us  [the longest x4 10.8 us: all_sum(): got_a = lax.ppermute(a, axes, first)]
    reduce_sum x1, other arithmetic: 9.75 us -> 27.5 us  [local(): sums_local = jnp.sum(flat, axis=0, dtype=jnp.float32)]
    ppermute x0 -> x10, starting transfers between devices: none -> 17.4 us  [the longest x4 11.5 us: all_sum(): got_a = lax.ppermute(a, axes, first)]
    dot_general x11 -> x0, matrix products: 15.2 us -> none  [the longest x4 7.72 us: local(): basis = orthonormal(jnp.dot(cov, basis, precision=lax.Precision.HIGHEST))]
  transfers between devices with their start and end apart: 5 -> 14, of which waited for: 3 -> 11; matrix products, arithmetic and copies ran while one was open for 2% -> 4% of each run, Pallas kernels for 0% -> 0%
where the time goes in v1:
time: 133 us; the launch traced here: 132 us
  other arithmetic  42.6 us (32%)
  starting transfers between devices  26.1 us (20%)
  waiting for transfers between devices  25 us (19%)
  Pallas kernels  22 us (17%)
  local copies, waits for them, and re-layouts  12.1 us (9%)
  matrix products  3.42 us (3%)
    reduce_sum x1, other arithmetic, local(): sums_local = jnp.sum(flat, axis=0, dtype=jnp.float32)  27.5 us
    pallas_call x1, Pallas kernels, components(): pl.pallas_call(functools.partial(components_kernel, count), out_shape=(ja...  22 us
    ppermute x4, starting transfers between devices, all_sum(): got_a = lax.ppermute(a, axes, first)  11.5 us
    ppermute x4, waiting for transfers between devices, all_sum(): got_a = lax.ppermute(a, axes, first)  10.8 us
    unnamed x12, local copies, waits for them, and re-layouts  10.2 us
    add x1, other arithmetic, along_rows(): total + GAUSS[offset] * padded[offset:offset + count].astype(jnp.float32)  8.36 us
    ppermute x2, starting transfers between devices, padded_2(): before = lax.ppermute(last, axis, up)  6.18 us
    ppermute x4, waiting for transfers between devices, all_sum(): got_b = lax.ppermute(b, axes, second)  5.46 us
  transfers between devices with their start and end apart: 14, of which 11 were waited for; matrix products, arithmetic and copies ran while one was open for 4% of the time, Pallas kernels for 0%

profile of v1, /device:TPU:0, one launch (start us, length us, event | category | flops | bytes accessed | tf_op | source)
XLA Modules:
  0.0 132.2 jit_solution(4136184429026644881)
XLA Ops:
  0.6 1.1 fusion.19
  1.7 4.9 %collective-permute-start = (bf16[2,128,384]{2,1,0:T(8,128)(2,1)S(1)}, bf16[2,128,384]{2,1,0:T(8,128)(2,1)S(1)}, u32[]{:S(2)}, u32[]{:S(2)}) collective-permute-start(bf16[2,128,384]{2,1,0:T(8,128)(2,1)S(1)} %get-tuple-element.14), channel_id=1, source_target_pairs={{0,4},{4,8},{8,12},{12,16},{16,20},{20,24},{24,28},{1,5},{5,9},{9,... | collective-permute-start | bytes 589832 | tf_op jit(solution)/shard_map/ppermute | solution.py:24
  6.6 1.3 collective-permute-start.1
  8.0 2.8 %collective-permute-done = bf16[2,128,384]{2,1,0:T(8,128)(2,1)S(1)} collective-permute-done((bf16[2,128,384]{2,1,0:T(8,128)(2,1)S(1)}, bf16[2,128,384]{2,1,0:T(8,128)(2,1)S(1)}, u32[]{:S(2)}, u32[]{:S(2)}) %collective-permute-start) | collective-permute-done | bytes 196640 | tf_op jit(solution)/shard_map/ppermute | solution.py:24
  10.8 4.6 %constant_dynamic-update-slice_fusion.1 = bf16[68,128,384]{2,1,0:T(8,128)(2,1)S(1)} fusion(bf16[68,128,384]{2,1,0:T(8,128)(2,1)S(1)} %constant_dynamic-update-slice_fusion.2, bf16[64,128,384]{2,1,0:T(8,128)(2,1)} %param.2), kind=kLoop, calls=%fused_computation.31 | loop fusion | bytes 12582912
  15.6 1.3 collective-permute-start.2
  16.9 1.3 collective-permute-start.3
  18.3 3.6 %collective-permute-done.3 = bf16[68,2,384]{2,1,0:T(2,128)(2,1)S(1)} collective-permute-done((bf16[68,2,384]{2,1,0:T(2,128)(2,1)S(1)}, bf16[68,2,384]{2,1,0:T(2,128)(2,1)S(1)}, u32[]{:S(2)}, u32[]{:S(2)}) %collective-permute-start.3) | collective-permute-done | bytes 104480 | tf_op jit(solution)/shard_map/ppermute | solution.py:25
  21.9 3.6 %pad_maximum_fusion = bf16[68,132,384]{2,1,0:T(8,128)(2,1)S(1)} fusion(bf16[68,2,384]{2,1,0:T(2,128)(2,1)S(1)} %collective-permute-done.3, bf16[68,128,384]{2,1,0:T(8,128)(2,1)S(1)} %constant_dynamic-update-slice_fusion, bf16[68,2,384]{2,1,0:T(2,128)(2,1)S(1)} %collective-permute-done.2), kind=kLoop, calls=%fused_computation.13 | loop fusion | flops 20680704 | bytes 13787136 | tf_op jit(solution)/shard_map/concatenate | solution.py:26
  25.5 8.4 %multiply_add_fusion = f32[64,132,384]{2,1,0:T(8,128)} fusion(bf16[68,132,384]{2,1,0:T(8,128)(2,1)S(1)} %pad_maximum_fusion), kind=kLoop, calls=%fused_computation | loop fusion | flops 45416448 | bytes 45416448 | tf_op jit(solution)/shard_map/add | solution.py:42
  33.9 27.5 %convert_reduce_fusion = (f32[384]{0:T(512)S(1)}, bf16[64,128,384]{2,1,0:T(8,128)(2,1)S(1)}) fusion(f32[64,128]{1,0:T(8,128)S(1)} %broadcast_multiply_fusion, f32[64,132,384]{2,1,0:T(8,128)} %multiply_add_fusion), kind=kLoop, calls=%fused_computation.11 | loop fusion | flops 40894080 | bytes 69240320 | tf_op jit(solution)/shard_map/reduce_sum | solution.py:236
  62.0 3.4 %convolution_bitcast_fusion = f32[384,384]{1,0:T(8,128)S(1)} fusion(bf16[64,128,384]{2,1,0:T(8,128)(2,1)S(1)} %get-tuple-element.10.smooth_hbm), kind=kOutput, calls=%fused_computation.14 | convolution fusion | flops 2415919104 | bytes 6881280 | tf_op jit(solution)/shard_map/dot_general | solution.py:233
  65.5 2.7 %copy-done = bf16[64,128,384]{2,1,0:T(8,128)(2,1)} copy-done((bf16[64,128,384]{2,1,0:T(8,128)(2,1)}, bf16[64,128,384]{2,1,0:T(8,128)(2,1)S(1)}, u32[]{:S(2)}) %copy-start) | copy-done | bytes 6291480
  68.1 0.7 fusion.6
  68.9 0.7 fusion.7
  69.7 0.7 fusion.8
  70.4 3.4 %collective-permute-start.4 = (f32[384,128]{1,0:T(8,128)S(1)}, f32[384,128]{1,0:T(8,128)S(1)}, u32[]{:S(2)}, u32[]{:S(2)}) collective-permute-start(f32[384,128]{1,0:T(8,128)S(1)} %constant_dynamic-slice_fusion), channel_id=1, source_target_pairs={{0,1},{1,0},{2,3},{3,2},{4,5},{5,4},{6,7},{7,6},{8,9},{9,8},{10,11... | collective-permute-start | bytes 589832 | tf_op jit(solution)/shard_map/ppermute | solution.py:83
  73.8 1.1 collective-permute-done.4
  74.9 6.7 %collective-permute-start.5 = (f32[192,128]{1,0:T(8,128)S(1)}, f32[192,128]{1,0:T(8,128)S(1)}, u32[]{:S(2)}, u32[]{:S(2)}) collective-permute-start(f32[192,128]{1,0:T(8,128)S(1)} %get-tuple-element.17), channel_id=1, source_target_pairs={{0,4},{1,5},{2,6},{3,7},{4,0},{5,1},{6,2},{7,3},{8,12},{9,13},{10,... | collective-permute-start | bytes 294920 | tf_op jit(solution)/shard_map/ppermute | solution.py:93
  81.8 3.2 %collective-permute-done.5 = f32[192,128]{1,0:T(8,128)S(1)} collective-permute-done((f32[192,128]{1,0:T(8,128)S(1)}, f32[192,128]{1,0:T(8,128)S(1)}, u32[]{:S(2)}, u32[]{:S(2)}) %collective-permute-start.5) | collective-permute-done | bytes 98336 | tf_op jit(solution)/shard_map/ppermute | solution.py:93
  84.9 1.5 %collective-permute-done.9 = f32[192,128]{1,0:T(8,128)S(1)} collective-permute-done((f32[192,128]{1,0:T(8,128)S(1)}, f32[192,128]{1,0:T(8,128)S(1)}, u32[]{:S(2)}, u32[]{:S(2)}) %collective-permute-start.9) | collective-permute-done | bytes 98336 | tf_op jit(solution)/shard_map/ppermute | solution.py:94
  87.1 4.0 %collective-permute-done.6 = f32[192,128]{1,0:T(8,128)S(1)} collective-permute-done((f32[192,128]{1,0:T(8,128)S(1)}, f32[192,128]{1,0:T(8,128)S(1)}, u32[]{:S(2)}, u32[]{:S(2)}) %collective-permute-start.6) | collective-permute-done | bytes 98336 | tf_op jit(solution)/shard_map/ppermute | solution.py:93
  91.1 1.6 %collective-permute-start.7 = (f32[192,128]{1,0:T(8,128)S(1)}, f32[192,128]{1,0:T(8,128)S(1)}, u32[]{:S(2)}, u32[]{:S(2)}) collective-permute-start(f32[192,128]{1,0:T(8,128)S(1)} %add.252), channel_id=1, source_target_pairs={{0,8},{1,9},{2,10},{3,11},{4,12},{5,13},{6,14},{7,15},{8,0},{9,1},... | collective-permute-start | bytes 294920 | tf_op jit(solution)/shard_map/ppermute | solution.py:93
  92.8 1.3 collective-permute-start.11
  94.1 2.0 %collective-permute-done.7 = f32[192,128]{1,0:T(8,128)S(1)} collective-permute-done((f32[192,128]{1,0:T(8,128)S(1)}, f32[192,128]{1,0:T(8,128)S(1)}, u32[]{:S(2)}, u32[]{:S(2)}) %collective-permute-start.7) | collective-permute-done | bytes 98336 | tf_op jit(solution)/shard_map/ppermute | solution.py:93
  96.1 2.9 %collective-permute-start.8 = (f32[192,128]{1,0:T(8,128)S(1)}, f32[192,128]{1,0:T(8,128)S(1)}, u32[]{:S(2)}, u32[]{:S(2)}) collective-permute-start(f32[192,128]{1,0:T(8,128)S(1)} %add.253), channel_id=1, source_target_pairs={{0,16},{1,17},{2,18},{3,19},{4,20},{5,21},{6,22},{7,23},{8,24},{9,... | collective-permute-start | bytes 294920 | tf_op jit(solution)/shard_map/ppermute | solution.py:93
  99.0 1.5 %collective-permute-done.11 = f32[192,128]{1,0:T(8,128)S(1)} collective-permute-done((f32[192,128]{1,0:T(8,128)S(1)}, f32[192,128]{1,0:T(8,128)S(1)}, u32[]{:S(2)}, u32[]{:S(2)}) %collective-permute-start.11) | collective-permute-done | bytes 98336 | tf_op jit(solution)/shard_map/ppermute | solution.py:94
  101.1 1.6 %collective-permute-done.8 = f32[192,128]{1,0:T(8,128)S(1)} collective-permute-done((f32[192,128]{1,0:T(8,128)S(1)}, f32[192,128]{1,0:T(8,128)S(1)}, u32[]{:S(2)}, u32[]{:S(2)}) %collective-permute-start.8) | collective-permute-done | bytes 98336 | tf_op jit(solution)/shard_map/ppermute | solution.py:93
  102.8 2.5 %collective-permute-done.12 = f32[192,128]{1,0:T(8,128)S(1)} collective-permute-done((f32[192,128]{1,0:T(8,128)S(1)}, f32[192,128]{1,0:T(8,128)S(1)}, u32[]{:S(2)}, u32[]{:S(2)}) %collective-permute-start.12) | collective-permute-done | bytes 98336 | tf_op jit(solution)/shard_map/ppermute | solution.py:94
  105.5 1.3 collective-permute-done.13
  106.8 2.8 %copy-done.1 = bf16[64,128,384]{2,1,0:T(8,128)(2,1)S(1)} copy-done((bf16[64,128,384]{2,1,0:T(8,128)(2,1)S(1)}, bf16[64,128,384]{2,1,0:T(8,128)(2,1)}, u32[]{:S(2)}) %copy-start.1) | copy-done | bytes 6291480
  109.6 22.0 %components.1 = (f32[1,384]{1,0:T(1,128)S(1)}, f32[384,384]{1,0:T(8,128)}, f32[64,64,128]{2,1,0:T(8,128)}) custom-call(f32[768,128]{1,0:T(8,128)S(1)} %maximum_select_fusion.packed, f32[384,64]{1,0:T(8,128)S(1)} %copy.6.start, bf16[64,128,384]{2,1,0:T(8,128)(2,1)S(1)} %copy-done.1), custom_call_target="tpu_custom_call" | custom-call | flops 1000000000 | bytes 10000000 | tf_op jit(solution)/shard_map/components/pallas_call | solution.py:200
  (39 shorter events, 3.4 us)
Async XLA Ops:
  1.7 9.1 %collective-permute-start = (bf16[2,128,384]{2,1,0:T(8,128)(2,1)S(1)}, bf16[2,128,384]{2,1,0:T(8,128)(2,1)S(1)}, u32[]{:S(2)}, u32[]{:S(2)}) collective-permute-start(bf16[2,128,384]{2,1,0:T(8,128)(2,1)S(1)} %get-tuple-element.14), channel_id=1, source_target_pairs={{0,4},{4,8},{8,12},{12,16},{16,20},{20,24},{24,28},{1,5},{5,9},{9,... | collective-permute-start | bytes 589832 | tf_op jit(solution)/shard_map/ppermute | solution.py:24
  6.6 8.8 %collective-permute-start.1 = (bf16[2,128,384]{2,1,0:T(8,128)(2,1)S(1)}, bf16[2,128,384]{2,1,0:T(8,128)(2,1)S(1)}, u32[]{:S(2)}, u32[]{:S(2)}) collective-permute-start(bf16[2,128,384]{2,1,0:T(8,128)(2,1)S(1)} %get-tuple-element.13), channel_id=1, source_target_pairs={{4,0},{8,4},{12,8},{16,12},{20,16},{24,20},{28,24},{5,1},{9,5},{13... | collective-permute-start | bytes 589832 | tf_op jit(solution)/shard_map/ppermute | solution.py:25
  15.6 2.6 %collective-permute-start.2 = (bf16[68,2,384]{2,1,0:T(2,128)(2,1)S(1)}, bf16[68,2,384]{2,1,0:T(2,128)(2,1)S(1)}, u32[]{:S(2)}, u32[]{:S(2)}) collective-permute-start(bf16[68,2,384]{2,1,0:T(2,128)(2,1)S(1)} %get-tuple-element.11), channel_id=1, source_target_pairs={{0,1},{1,2},{2,3},{4,5},{5,6},{6,7},{8,9},{9,10},{10,11},{12,13},{... | collective-permute-start | bytes 313352 | tf_op jit(solution)/shard_map/ppermute | solution.py:24
  16.9 5.0 %collective-permute-start.3 = (bf16[68,2,384]{2,1,0:T(2,128)(2,1)S(1)}, bf16[68,2,384]{2,1,0:T(2,128)(2,1)S(1)}, u32[]{:S(2)}, u32[]{:S(2)}) collective-permute-start(bf16[68,2,384]{2,1,0:T(2,128)(2,1)S(1)} %get-tuple-element.12), channel_id=1, source_target_pairs={{1,0},{2,1},{3,2},{5,4},{6,5},{7,6},{9,8},{10,9},{11,10},{13,12},{... | collective-permute-start | bytes 313352 | tf_op jit(solution)/shard_map/ppermute | solution.py:25
  61.4 43.9 %copy-start.2 = (f32[384,64]{0,1:T(8,128)S(1)}, f32[384,64]{0,1:T(8,128)}, u32[]{:S(2)}) copy-start(f32[384,64]{0,1:T(8,128)} %param.3) | copy-start | bytes 294916
  65.4 2.7 %copy-start = (bf16[64,128,384]{2,1,0:T(8,128)(2,1)}, bf16[64,128,384]{2,1,0:T(8,128)(2,1)S(1)}, u32[]{:S(2)}) copy-start(bf16[64,128,384]{2,1,0:T(8,128)(2,1)S(1)} %get-tuple-element.10.smooth_hbm) | copy-start | bytes 18874372
  70.4 4.4 %collective-permute-start.4 = (f32[384,128]{1,0:T(8,128)S(1)}, f32[384,128]{1,0:T(8,128)S(1)}, u32[]{:S(2)}, u32[]{:S(2)}) collective-permute-start(f32[384,128]{1,0:T(8,128)S(1)} %constant_dynamic-slice_fusion), channel_id=1, source_target_pairs={{0,1},{1,0},{2,3},{3,2},{4,5},{5,4},{6,7},{7,6},{8,9},{9,8},{10,11... | collective-permute-start | bytes 589832 | tf_op jit(solution)/shard_map/ppermute | solution.py:83
  74.9 10.0 %collective-permute-start.5 = (f32[192,128]{1,0:T(8,128)S(1)}, f32[192,128]{1,0:T(8,128)S(1)}, u32[]{:S(2)}, u32[]{:S(2)}) collective-permute-start(f32[192,128]{1,0:T(8,128)S(1)} %get-tuple-element.17), channel_id=1, source_target_pairs={{0,4},{1,5},{2,6},{3,7},{4,0},{5,1},{6,2},{7,3},{8,12},{9,13},{10,... | collective-permute-start | bytes 294920 | tf_op jit(solution)/shard_map/ppermute | solution.py:93
  81.6 4.8 %collective-permute-start.9 = (f32[192,128]{1,0:T(8,128)S(1)}, f32[192,128]{1,0:T(8,128)S(1)}, u32[]{:S(2)}, u32[]{:S(2)}) collective-permute-start(f32[192,128]{1,0:T(8,128)S(1)} %get-tuple-element.18), channel_id=1, source_target_pairs={{0,2},{1,3},{2,0},{3,1},{4,6},{5,7},{6,4},{7,5},{8,10},{9,11},{10,... | collective-permute-start | bytes 294920 | tf_op jit(solution)/shard_map/ppermute | solution.py:94
  86.4 4.7 %collective-permute-start.6 = (f32[192,128]{1,0:T(8,128)S(1)}, f32[192,128]{1,0:T(8,128)S(1)}, u32[]{:S(2)}, u32[]{:S(2)}) collective-permute-start(f32[192,128]{1,0:T(8,128)S(1)} %get-tuple-element.15), channel_id=1, source_target_pairs={{0,2},{1,3},{2,0},{3,1},{4,6},{5,7},{6,4},{7,5},{8,10},{9,11},{10,... | collective-permute-start | bytes 294920 | tf_op jit(solution)/shard_map/ppermute | solution.py:93
  86.8 6.0 %collective-permute-start.10 = (f32[192,128]{1,0:T(8,128)S(1)}, f32[192,128]{1,0:T(8,128)S(1)}, u32[]{:S(2)}, u32[]{:S(2)}) collective-permute-start(f32[192,128]{1,0:T(8,128)S(1)} %get-tuple-element.16), channel_id=1, source_target_pairs={{0,4},{1,5},{2,6},{3,7},{4,0},{5,1},{6,2},{7,3},{8,12},{9,13},{10,... | collective-permute-start | bytes 294920 | tf_op jit(solution)/shard_map/ppermute | solution.py:94
  91.1 5.0 %collective-permute-start.7 = (f32[192,128]{1,0:T(8,128)S(1)}, f32[192,128]{1,0:T(8,128)S(1)}, u32[]{:S(2)}, u32[]{:S(2)}) collective-permute-start(f32[192,128]{1,0:T(8,128)S(1)} %add.252), channel_id=1, source_target_pairs={{0,8},{1,9},{2,10},{3,11},{4,12},{5,13},{6,14},{7,15},{8,0},{9,1},... | collective-permute-start | bytes 294920 | tf_op jit(solution)/shard_map/ppermute | solution.py:93
  92.8 7.7 %collective-permute-start.11 = (f32[192,128]{1,0:T(8,128)S(1)}, f32[192,128]{1,0:T(8,128)S(1)}, u32[]{:S(2)}, u32[]{:S(2)}) collective-permute-start(f32[192,128]{1,0:T(8,128)S(1)} %add.256), channel_id=1, source_target_pairs={{0,16},{1,17},{2,18},{3,19},{4,20},{5,21},{6,22},{7,23},{8,24},{9,... | collective-permute-start | bytes 294920 | tf_op jit(solution)/shard_map/ppermute | solution.py:94
  96.1 6.6 %collective-permute-start.8 = (f32[192,128]{1,0:T(8,128)S(1)}, f32[192,128]{1,0:T(8,128)S(1)}, u32[]{:S(2)}, u32[]{:S(2)}) collective-permute-start(f32[192,128]{1,0:T(8,128)S(1)} %add.253), channel_id=1, source_target_pairs={{0,16},{1,17},{2,18},{3,19},{4,20},{5,21},{6,22},{7,23},{8,24},{9,... | collective-permute-start | bytes 294920 | tf_op jit(solution)/shard_map/ppermute | solution.py:93
  100.5 4.7 %collective-permute-start.12 = (f32[192,128]{1,0:T(8,128)S(1)}, f32[192,128]{1,0:T(8,128)S(1)}, u32[]{:S(2)}, u32[]{:S(2)}) collective-permute-start(f32[192,128]{1,0:T(8,128)S(1)} %add.257), channel_id=1, source_target_pairs={{0,8},{1,9},{2,10},{3,11},{4,12},{5,13},{6,14},{7,15},{8,0},{9,1},... | collective-permute-start | bytes 294920 | tf_op jit(solution)/shard_map/ppermute | solution.py:94
  105.3 1.5 %collective-permute-start.13 = (f32[384,128]{1,0:T(8,128)S(1)}, f32[384,128]{1,0:T(8,128)S(1)}, u32[]{:S(2)}, u32[]{:S(2)}) collective-permute-start(f32[384,128]{1,0:T(8,128)S(1)} %pad_maximum_fusion.1), channel_id=1, source_target_pairs={{0,1},{1,0},{2,3},{3,2},{4,5},{5,4},{6,7},{7,6},{8,9},{9,8},{10,11... | collective-permute-start | bytes 589832 | tf_op jit(solution)/shard_map/ppermute | solution.py:98
  106.8 2.8 %copy-start.1 = (bf16[64,128,384]{2,1,0:T(8,128)(2,1)S(1)}, bf16[64,128,384]{2,1,0:T(8,128)(2,1)}, u32[]{:S(2)}) copy-start(bf16[64,128,384]{2,1,0:T(8,128)(2,1)} %copy-done) | copy-start | bytes 18874372

commit v2 on v1

--- a/solution.py
+++ b/solution.py
@@ -14,17 +14,17 @@
 GAUSS = (0.0625, 0.25, 0.375, 0.25, 0.0625)
 
 
-def padded_2(shard, sides, width):
-    for axis, dim in sides:
-        size, length = (lax.axis_size(axis), shard.shape[dim])
-        up = [(i, (i + 1) % size) for i in range(size - 1)]
-        down = [(j, i) for i, j in up]
-        last = lax.slice_in_dim(shard, length - width, length, axis=dim)
-        first = lax.slice_in_dim(shard, 0, width, axis=dim)
-        before = lax.ppermute(last, axis, up)
-        after = lax.ppermute(first, axis, down)
-        shard = jnp.concatenate([before, shard, after], axis=dim)
-    return shard
+WIDTH = 2
+HALO_ROWS = 16
+
+
+def edges_2(shard, axis, dim):
+    size, length = (lax.axis_size(axis), shard.shape[dim])
+    up = [(i, i + 1) for i in range(size - 1)]
+    down = [(j, i) for i, j in up]
+    before = lax.ppermute(lax.slice_in_dim(shard, length - WIDTH, length, axis=dim), axis, up)
+    after = lax.ppermute(lax.slice_in_dim(shard, 0, WIDTH, axis=dim), axis, down)
+    return before, after
 
 
 def edge_weight(first, count, total):
@@ -36,34 +36,137 @@
     return weight
 
 
-def along_rows(padded, count):
-    total = GAUSS[0] * padded[0:count].astype(jnp.float32)
-    for offset in range(1, 5):
-        total = total + GAUSS[offset] * padded[offset : offset + count].astype(jnp.float32)
-    return total
-
-
-def along_cols(padded, count):
-    total = GAUSS[0] * padded[:, 0:count]
-    for offset in range(1, 5):
-        total = total + GAUSS[offset] * padded[:, offset : offset + count]
-    return total
-
-
-def pack_gram(gram, sums):
-    n = gram.shape[0] // LANES
+def column_taps(count):
+    out = jnp.arange(count, dtype=jnp.int32)[:, None]
+    k = jnp.arange(count + HALO_ROWS, dtype=jnp.int32)[None, :]
+    beside = k - count
+    place = jnp.where(k < count, k, jnp.where(beside < WIDTH, beside - WIDTH, count + beside - WIDTH))
+    place = jnp.where(beside < 2 * WIDTH, place, -count)
+    taps = jnp.zeros((count, count + HALO_ROWS), jnp.float32)
+    for offset in range(5):
+        taps = jnp.where(place == out + offset - 2, GAUSS[offset], taps)
+    return taps.astype(jnp.bfloat16)
+
+
+def smooth_kernel(
+    row_scale, pixels, above, below, left, right, taps, col_scale, smooth_hbm, packed,
+    source, across, smooth, gram, sums, in_sem, out_sem,
+):
+    tile_rows, tile_cols, feat = pixels.shape
+    group = 8
+    groups = tile_rows // group
+    span = tile_cols + HALO_ROWS
+
+    def fetch(g):
+        rows = pl.ds(g * group, group)
+        there = source.at[pl.ds(g * group + WIDTH, group), pl.ds(0, tile_cols), :]
+        return pltpu.make_async_copy(pixels.at[rows], there, in_sem.at[g])
+
+    for g in range(groups):
+        fetch(g).start()
+    source[:, tile_cols:span, :] = jnp.zeros((tile_rows + 2 * WIDTH, HALO_ROWS, feat), jnp.bfloat16)
+    source[0:WIDTH, 0:tile_cols, :] = above[...]
+    source[tile_rows + WIDTH :, 0:tile_cols, :] = below[...]
+    source[:, tile_cols : tile_cols + WIDTH, :] = left[...]
+    source[:, tile_cols + WIDTH : tile_cols + 2 * WIDTH, :] = right[...]
+    gram[...] = jnp.zeros_like(gram)
+    sums[...] = jnp.zeros_like(sums)
+    b = taps[...]
+
+    def horizontal(r):
+        across[r] = jnp.dot(b, source[r], preferred_element_type=jnp.float32)
+
+    def vertical(g):
+        sub = 16
+        for i in range(tile_cols // sub):
+            at = pl.ds(i * sub, sub)
+            for f in range(feat // LANES):
+                lanes = pl.ds(f * LANES, LANES)
+                scale = col_scale[at, :]
+                c = [across[g * group + r, at, lanes] for r in range(group + 4)]
+                total = None
+                for r in range(group):
+                    v = c[r] + c[r + 4] + 4.0 * (c[r + 1] + c[r + 3]) + 6.0 * c[r + 2]
+                    v = (v * (scale * row_scale[g * group + r])).astype(jnp.bfloat16)
+                    smooth[g * group + r, at, lanes] = v
+                    v = v.astype(jnp.float32)
+                    total = v if total is None else total + v
+                sums[:, lanes] += total
+
+    def correlate(g):
+        s = smooth[pl.ds(g * group, group)].reshape(group * tile_cols, feat)
+        over = (((0,), (0,)), ((), ()))
+        wide = feat - LANES
+        gram[0:wide, 0:wide] += lax.dot_general(s[:, :wide], s[:, :wide], over, preferred_element_type=jnp.float32)
+        gram[:, wide:] += lax.dot_general(s, s[:, wide:], over, preferred_element_type=jnp.float32)
+
+    def send(g):
+        rows = pl.ds(g * group, group)
+        return pltpu.make_async_copy(smooth.at[rows], smooth_hbm.at[rows], out_sem.at[g])
+
+    for r in range(WIDTH):
+        horizontal(r)
+        horizontal(tile_rows + WIDTH + r)
+    fetch(0).wait()
+    for r in range(group):
+        horizontal(WIDTH + r)
+
+    @pl.loop(0, groups)
+    def _(g):
+        @pl.when(g < groups - 1)
+        def _():
+            fetch(g + 1).wait()
+            for r in range(group):
+                horizontal((g + 1) * group + WIDTH + r)
+
+        vertical(g)
+        correlate(g)
+        send(g).start()
+
     row = lax.broadcasted_iota(jnp.int32, (LANES, LANES), 0)
     col = lax.broadcasted_iota(jnp.int32, (LANES, LANES), 1)
-    blocks = []
+    n = feat // LANES
+    at = 0
     for i in range(n):
         for j in range(i, n):
             block = gram[i * LANES : (i + 1) * LANES, j * LANES : (j + 1) * LANES]
             if i == j:
-                piece = sums[i * LANES : (i + 1) * LANES]
-                block = jnp.where((row == LANES - 1) & (col < LANES - 1), piece[None, :], block)
-                block = jnp.where((row == LANES - 2) & (col == 0), piece[LANES - 1], block)
-            blocks.append(block)
-    return jnp.concatenate(blocks, axis=0)
+                piece = jnp.sum(sums[:, i * LANES : (i + 1) * LANES], axis=0, keepdims=True)
+                block = jnp.where((row == LANES - 1) & (col < LANES - 1), piece, block)
+                block = jnp.where((row == LANES - 2) & (col == 0), piece[:, LANES - 1 : LANES], block)
+            packed[at * LANES : (at + 1) * LANES, :] = block
+            at += 1
+    for g in range(groups):
+        send(g).wait()
+
+
+def smooth_and_gram(pixels, above, below, left, right, taps, row_scale, col_scale):
+    tile_rows, tile_cols, feat = pixels.shape
+    n = feat // LANES
+    vmem = pl.BlockSpec(memory_space=pltpu.VMEM)
+    hbm = pl.BlockSpec(memory_space=pl.ANY)
+    smem = pl.BlockSpec(memory_space=pltpu.SMEM)
+    return pl.pallas_call(
+        smooth_kernel,
+        out_shape=(
+            jax.ShapeDtypeStruct(pixels.shape, jnp.bfloat16),
+            jax.ShapeDtypeStruct((n * (n + 1) // 2 * LANES, LANES), jnp.float32),
+        ),
+        in_specs=[smem, hbm, vmem, vmem, vmem, vmem, vmem, vmem],
+        out_specs=(hbm, vmem),
+        scratch_shapes=[
+            pltpu.VMEM((tile_rows + 4, tile_cols + HALO_ROWS, feat), jnp.bfloat16),
+            pltpu.VMEM((tile_rows + 4, tile_cols, feat), jnp.float32),
+            pltpu.VMEM(pixels.shape, jnp.bfloat16),
+            pltpu.VMEM((feat, feat), jnp.float32),
+            pltpu.VMEM((16, feat), jnp.float32),
+            pltpu.SemaphoreType.DMA((tile_rows // 8,)),
+            pltpu.SemaphoreType.DMA((tile_rows // 8,)),
+        ],
+        compiler_params=pltpu.CompilerParams(vmem_limit_bytes=40 << 20),
+        cost_estimate=pl.CostEstimate(flops=5 * 10**9, bytes_accessed=2 * 10**7, transcendentals=0),
+        name="smooth",
+    )(row_scale, pixels, above, below, left, right, taps, col_scale)
 
 
 def all_sum(values):
@@ -223,18 +326,18 @@
     tile_rows, tile_cols, feat = pixels.shape
     rows_total = tile_rows * lax.axis_size("row")
     cols_total = tile_cols * lax.axis_size("col")
-    padded = padded_2(pixels, (("row", 0), ("col", 1)), 2)
-    blurred = along_cols(along_rows(padded, tile_rows), tile_cols)
-    row_weight = edge_weight(lax.axis_index("row") * tile_rows, tile_rows, rows_total)
-    col_weight = edge_weight(lax.axis_index("col") * tile_cols, tile_cols, cols_total)
-    weight = row_weight[:, None, None] * col_weight[None, :, None]
-    smoothed = (blurred / weight).astype(jnp.bfloat16)
-    flat = smoothed.reshape(tile_rows * tile_cols, feat)
-    gram_local = lax.dot_general(
-        flat, flat, (((0,), (0,)), ((), ())), preferred_element_type=jnp.float32
+    above, below = edges_2(pixels, "row", 0)
+    beside = [jnp.concatenate([above[:, c], pixels[:, c], below[:, c]], axis=0) for c in (slice(0, WIDTH), slice(tile_cols - WIDTH, tile_cols))]
+    size = lax.axis_size("col")
+    left = lax.ppermute(beside[1], "col", [(i, i + 1) for i in range(size - 1)])
+    right = lax.ppermute(beside[0], "col", [(i + 1, i) for i in range(size - 1)])
+    row_scale = GAUSS[0] / edge_weight(lax.axis_index("row") * tile_rows, tile_rows, rows_total)
+    col_scale = 1.0 / edge_weight(lax.axis_index("col") * tile_cols, tile_cols, cols_total)
+    col_scale = jnp.broadcast_to(col_scale[:, None], (tile_cols, LANES))
+    smoothed, packed = smooth_and_gram(
+        pixels, above, below, left, right, column_taps(tile_cols), row_scale, col_scale
     )
-    sums_local = jnp.sum(flat, axis=0, dtype=jnp.float32)
-    packed = all_sum(pack_gram(gram_local, sums_local))
+    packed = all_sum(packed)
     mean, projector, scores = components(packed, start, smoothed, float(rows_total * cols_total))
     return (mean.reshape(feat), projector, scores)
 

time: 133 us -> 99.7 us (0.75)
  other arithmetic: 42.6 us -> 1.24 us
  Pallas kernels: 22 us -> 35.8 us
  matrix products: 3.42 us -> 0 us
  starting transfers between devices: 26.1 us -> 23.3 us
  waiting for transfers between devices: 25 us -> 27.4 us
    reduce_sum x1 -> x0, other arithmetic: 27.5 us -> none  [local(): sums_local = jnp.sum(flat, axis=0, dtype=jnp.float32)]
    pallas_call x0 -> x1, Pallas kernels: none -> 13.8 us  [smooth_and_gram(): pl.pallas_call(smooth_kernel, out_shape=(jax.ShapeDtypeStruct(pixels.shap...]
    add x3 -> x0, other arithmetic: 8.38 us -> none  [the longest x1 8.36 us: along_rows(): total + GAUSS[offset] * padded[offset:offset + count].astype(jnp.float32)]
    ppermute x4, starting transfers between devices: 11.5 us -> 7.4 us  [all_sum(): got_a = lax.ppermute(a, axes, first)]
    concatenate x2, other arithmetic: 4.36 us -> 0.31 us  [local(): jnp.concatenate([above[:, c], pixels[:, c], below[:, c]], axis=0)]
    dot_general x1 -> x0, matrix products: 3.42 us -> none  [local(): lax.dot_general(flat, flat, (((0,), (0,)), ((), ())), preferred_element_t...]
    ppermute x4, waiting for transfers between devices: 6.4 us -> 8.78 us  [the longest x1 4.35 us: edges_2(): lax.ppermute(lax.slice_in_dim(shard, length - WIDTH, length, axis=dim), a...]
    unnamed x12 -> x9, local copies, waits for them, and re-layouts: 10.2 us -> 8.34 us
  transfers between devices with their start and end apart: 14 -> 14, of which waited for: 11 -> 12; matrix products, arithmetic and copies ran while one was open for 4% -> 2% of each run, Pallas kernels for 0% -> 0%
where the time goes in v2:
time: 99.7 us; the launch traced here: 99.4 us
  Pallas kernels  35.8 us (36%)
  waiting for transfers between devices  27.4 us (27%)
  starting transfers between devices  23.3 us (23%)
  local copies, waits for them, and re-layouts  10.8 us (11%)
  other arithmetic  1.24 us (1%)
    pallas_call x1, Pallas kernels, components(): pl.pallas_call(functools.partial(components_kernel, count), out_shape=(ja...  22 us
    pallas_call x1, Pallas kernels, smooth_and_gram(): pl.pallas_call(smooth_kernel, out_shape=(jax.ShapeDtypeStruct(pixels.shap...  13.8 us
    ppermute x4, waiting for transfers between devices, all_sum(): got_a = lax.ppermute(a, axes, first)  10.8 us
    unnamed x9, local copies, waits for them, and re-layouts  8.34 us
    ppermute x4, starting transfers between devices, all_sum(): got_a = lax.ppermute(a, axes, first)  7.4 us
    ppermute x1, starting transfers between devices, edges_2(): lax.ppermute(lax.slice_in_dim(shard, length - WIDTH, length, axis=dim), a...  5.51 us
    ppermute x4, waiting for transfers between devices, all_sum(): got_b = lax.ppermute(b, axes, second)  5.46 us
    ppermute x1, waiting for transfers between devices, edges_2(): lax.ppermute(lax.slice_in_dim(shard, length - WIDTH, length, axis=dim), a...  4.35 us
  transfers between devices with their start and end apart: 14, of which 12 were waited for; matrix products, arithmetic and copies ran while one was open for 2% of the time, Pallas kernels for 0%

profile of v2, /device:TPU:0, one launch (start us, length us, event | category | flops | bytes accessed | tf_op | source)
XLA Modules:
  0.0 99.4 jit_solution(8242781744248243672)
XLA Ops:
  0.6 1.1 %fusion.11 = (bf16[2,128,384]{2,1,0:T(8,128)(2,1)S(1)}, bf16[2,128,384]{2,1,0:T(8,128)(2,1)S(1)}) fusion(bf16[64,128,384]{2,1,0:T(8,128)(2,1)} %pixels.1), kind=kLoop, calls=%fused_computation.41 | loop fusion | bytes 786432 | tf_op jit(solution)/shard_map/slice | solution.py:26
  1.7 1.3 %collective-permute-start.1 = (bf16[2,128,384]{2,1,0:T(8,128)(2,1)S(1)}, bf16[2,128,384]{2,1,0:T(8,128)(2,1)S(1)}, u32[]{:S(2)}, u32[]{:S(2)}) collective-permute-start(bf16[2,128,384]{2,1,0:T(8,128)(2,1)S(1)} %get-tuple-element.15), channel_id=1, source_target_pairs={{4,0},{8,4},{12,8},{16,12},{20,16},{24,20},{28,24},{5,1},{9,5},{13... | collective-permute-start | bytes 589832 | tf_op jit(solution)/shard_map/ppermute | solution.py:26
  3.0 5.5 %collective-permute-start = (bf16[2,128,384]{2,1,0:T(8,128)(2,1)S(1)}, bf16[2,128,384]{2,1,0:T(8,128)(2,1)S(1)}, u32[]{:S(2)}, u32[]{:S(2)}) collective-permute-start(bf16[2,128,384]{2,1,0:T(8,128)(2,1)S(1)} %get-tuple-element.16), channel_id=1, source_target_pairs={{0,4},{4,8},{8,12},{12,16},{16,20},{20,24},{24,28},{1,5},{5,9},{9,... | collective-permute-start | bytes 589832 | tf_op jit(solution)/shard_map/ppermute | solution.py:25
  8.6 1.3 %fusion.10 = (bf16[64,2,384]{2,1,0:T(2,128)(2,1)S(1)}, bf16[64,2,384]{2,1,0:T(2,128)(2,1)S(1)}) fusion(bf16[64,128,384]{2,1,0:T(8,128)(2,1)} %pixels.1), kind=kLoop, calls=%fused_computation.40 | loop fusion | bytes 393216 | tf_op jit(solution)/shard_map/slice | solution.py:330
  10.0 1.4 %collective-permute-done.1.below = bf16[2,128,384]{2,1,0:T(8,128)(2,1)S(1)} collective-permute-done((bf16[2,128,384]{2,1,0:T(8,128)(2,1)S(1)}, bf16[2,128,384]{2,1,0:T(8,128)(2,1)S(1)}, u32[]{:S(2)}, u32[]{:S(2)}) %collective-permute-start.1) | collective-permute-done | bytes 196640 | tf_op jit(solution)/shard_map/ppermute | solution.py:26
  11.5 4.4 %collective-permute-done.above = bf16[2,128,384]{2,1,0:T(8,128)(2,1)S(1)} collective-permute-done((bf16[2,128,384]{2,1,0:T(8,128)(2,1)S(1)}, bf16[2,128,384]{2,1,0:T(8,128)(2,1)S(1)}, u32[]{:S(2)}, u32[]{:S(2)}) %collective-permute-start) | collective-permute-done | bytes 196640 | tf_op jit(solution)/shard_map/ppermute | solution.py:25
  16.0 1.9 %collective-permute-start.2 = (bf16[68,2,384]{2,1,0:T(2,128)(2,1)S(1)}, bf16[68,2,384]{2,1,0:T(2,128)(2,1)S(1)}, u32[]{:S(2)}, u32[]{:S(2)}) collective-permute-start(bf16[68,2,384]{2,1,0:T(2,128)(2,1)S(1)} %pad_maximum_fusion.1), channel_id=1, source_target_pairs={{0,1},{1,2},{2,3},{4,5},{5,6},{6,7},{8,9},{9,10},{10,11},{12,13},{... | collective-permute-start | bytes 313352 | tf_op jit(solution)/shard_map/ppermute | solution.py:332
  18.1 1.3 %collective-permute-start.3 = (bf16[68,2,384]{2,1,0:T(2,128)(2,1)S(1)}, bf16[68,2,384]{2,1,0:T(2,128)(2,1)S(1)}, u32[]{:S(2)}, u32[]{:S(2)}) collective-permute-start(bf16[68,2,384]{2,1,0:T(2,128)(2,1)S(1)} %pad_maximum_fusion.2), channel_id=1, source_target_pairs={{1,0},{2,1},{3,2},{5,4},{6,5},{7,6},{9,8},{10,9},{11,10},{13,12},{... | collective-permute-start | bytes 313352 | tf_op jit(solution)/shard_map/ppermute | solution.py:333
  19.4 3.0 %collective-permute-done.3.right = bf16[68,2,384]{2,1,0:T(2,128)(2,1)S(1)} collective-permute-done((bf16[68,2,384]{2,1,0:T(2,128)(2,1)S(1)}, bf16[68,2,384]{2,1,0:T(2,128)(2,1)S(1)}, u32[]{:S(2)}, u32[]{:S(2)}) %collective-permute-start.3) | collective-permute-done | bytes 104480 | tf_op jit(solution)/shard_map/ppermute | solution.py:333
  22.5 2.8 %copy-done.2 = bf16[64,128,384]{2,1,0:T(8,128)(2,1)S(1)} copy-done((bf16[64,128,384]{2,1,0:T(8,128)(2,1)S(1)}, bf16[64,128,384]{2,1,0:T(8,128)(2,1)}, u32[]{:S(2)}) %copy-start.2) | copy-done | bytes 6291480
  25.3 13.8 %smooth.1 = (bf16[64,128,384]{2,1,0:T(8,128)(2,1)S(1)}, f32[768,128]{1,0:T(8,128)S(1)}) custom-call(f32[64]{0:T(128)S(1)} %fusion.9.row_scale, bf16[64,128,384]{2,1,0:T(8,128)(2,1)S(1)} %copy-done.2, bf16[2,128,384]{2,1,0:T(8,128)(2,1)S(1)} %collective-permute-done.above, bf16[2,128,384]{2,1,0:T(8,128)(2,1)S(1)} %collective-permute-done.1.below, ...), custom_call_target="tpu_custom_call" | custom-call | flops 5000000000 | bytes 20000000 | tf_op jit(solution)/shard_map/smooth/pallas_call | solution.py:149
  39.1 2.6 %copy-done = bf16[64,128,384]{2,1,0:T(8,128)(2,1)} copy-done((bf16[64,128,384]{2,1,0:T(8,128)(2,1)}, bf16[64,128,384]{2,1,0:T(8,128)(2,1)S(1)}, u32[]{:S(2)}) %copy-start) | copy-done | bytes 6291480
  41.8 3.4 %collective-permute-start.4 = (f32[384,128]{1,0:T(8,128)S(1)}, f32[384,128]{1,0:T(8,128)S(1)}, u32[]{:S(2)}, u32[]{:S(2)}) collective-permute-start(f32[384,128]{1,0:T(8,128)S(1)} %constant_dynamic-slice_fusion), channel_id=1, source_target_pairs={{0,1},{1,0},{2,3},{3,2},{4,5},{5,4},{6,7},{7,6},{8,9},{9,8},{10,11... | collective-permute-start | bytes 589832 | tf_op jit(solution)/shard_map/ppermute | solution.py:186
  45.1 1.1 %collective-permute-done.4 = f32[384,128]{1,0:T(8,128)S(1)} collective-permute-done((f32[384,128]{1,0:T(8,128)S(1)}, f32[384,128]{1,0:T(8,128)S(1)}, u32[]{:S(2)}, u32[]{:S(2)}) %collective-permute-start.4) | collective-permute-done | bytes 196640 | tf_op jit(solution)/shard_map/ppermute | solution.py:186
  46.3 2.5 %collective-permute-start.5 = (f32[192,128]{1,0:T(8,128)S(1)}, f32[192,128]{1,0:T(8,128)S(1)}, u32[]{:S(2)}, u32[]{:S(2)}) collective-permute-start(f32[192,128]{1,0:T(8,128)S(1)} %get-tuple-element.19), channel_id=1, source_target_pairs={{0,4},{1,5},{2,6},{3,7},{4,0},{5,1},{6,2},{7,3},{8,12},{9,13},{10,... | collective-permute-start | bytes 294920 | tf_op jit(solution)/shard_map/ppermute | solution.py:196
  49.0 3.2 %collective-permute-done.5 = f32[192,128]{1,0:T(8,128)S(1)} collective-permute-done((f32[192,128]{1,0:T(8,128)S(1)}, f32[192,128]{1,0:T(8,128)S(1)}, u32[]{:S(2)}, u32[]{:S(2)}) %collective-permute-start.5) | collective-permute-done | bytes 98336 | tf_op jit(solution)/shard_map/ppermute | solution.py:196
  52.1 1.5 %collective-permute-done.9 = f32[192,128]{1,0:T(8,128)S(1)} collective-permute-done((f32[192,128]{1,0:T(8,128)S(1)}, f32[192,128]{1,0:T(8,128)S(1)}, u32[]{:S(2)}, u32[]{:S(2)}) %collective-permute-start.9) | collective-permute-done | bytes 98336 | tf_op jit(solution)/shard_map/ppermute | solution.py:197
  53.6 0.3 collective-permute-start.6
  54.0 0.4 collective-permute-start.10
  54.3 4.0 %collective-permute-done.6 = f32[192,128]{1,0:T(8,128)S(1)} collective-permute-done((f32[192,128]{1,0:T(8,128)S(1)}, f32[192,128]{1,0:T(8,128)S(1)}, u32[]{:S(2)}, u32[]{:S(2)}) %collective-permute-start.6) | collective-permute-done | bytes 98336 | tf_op jit(solution)/shard_map/ppermute | solution.py:196
  58.3 1.6 %collective-permute-start.7 = (f32[192,128]{1,0:T(8,128)S(1)}, f32[192,128]{1,0:T(8,128)S(1)}, u32[]{:S(2)}, u32[]{:S(2)}) collective-permute-start(f32[192,128]{1,0:T(8,128)S(1)} %add.257), channel_id=1, source_target_pairs={{0,8},{1,9},{2,10},{3,11},{4,12},{5,13},{6,14},{7,15},{8,0},{9,1},... | collective-permute-start | bytes 294920 | tf_op jit(solution)/shard_map/ppermute | solution.py:196
  60.0 1.3 %collective-permute-start.11 = (f32[192,128]{1,0:T(8,128)S(1)}, f32[192,128]{1,0:T(8,128)S(1)}, u32[]{:S(2)}, u32[]{:S(2)}) collective-permute-start(f32[192,128]{1,0:T(8,128)S(1)} %add.261), channel_id=1, source_target_pairs={{0,16},{1,17},{2,18},{3,19},{4,20},{5,21},{6,22},{7,23},{8,24},{9,... | collective-permute-start | bytes 294920 | tf_op jit(solution)/shard_map/ppermute | solution.py:197
  61.3 2.0 %collective-permute-done.7 = f32[192,128]{1,0:T(8,128)S(1)} collective-permute-done((f32[192,128]{1,0:T(8,128)S(1)}, f32[192,128]{1,0:T(8,128)S(1)}, u32[]{:S(2)}, u32[]{:S(2)}) %collective-permute-start.7) | collective-permute-done | bytes 98336 | tf_op jit(solution)/shard_map/ppermute | solution.py:196
  63.3 2.9 %collective-permute-start.8 = (f32[192,128]{1,0:T(8,128)S(1)}, f32[192,128]{1,0:T(8,128)S(1)}, u32[]{:S(2)}, u32[]{:S(2)}) collective-permute-start(f32[192,128]{1,0:T(8,128)S(1)} %add.258), channel_id=1, source_target_pairs={{0,16},{1,17},{2,18},{3,19},{4,20},{5,21},{6,22},{7,23},{8,24},{9,... | collective-permute-start | bytes 294920 | tf_op jit(solution)/shard_map/ppermute | solution.py:196
  66.2 1.5 %collective-permute-done.11 = f32[192,128]{1,0:T(8,128)S(1)} collective-permute-done((f32[192,128]{1,0:T(8,128)S(1)}, f32[192,128]{1,0:T(8,128)S(1)}, u32[]{:S(2)}, u32[]{:S(2)}) %collective-permute-start.11) | collective-permute-done | bytes 98336 | tf_op jit(solution)/shard_map/ppermute | solution.py:197
  67.7 0.6 collective-permute-start.12
  68.3 1.6 %collective-permute-done.8 = f32[192,128]{1,0:T(8,128)S(1)} collective-permute-done((f32[192,128]{1,0:T(8,128)S(1)}, f32[192,128]{1,0:T(8,128)S(1)}, u32[]{:S(2)}, u32[]{:S(2)}) %collective-permute-start.8) | collective-permute-done | bytes 98336 | tf_op jit(solution)/shard_map/ppermute | solution.py:196
  70.0 2.5 %collective-permute-done.12 = f32[192,128]{1,0:T(8,128)S(1)} collective-permute-done((f32[192,128]{1,0:T(8,128)S(1)}, f32[192,128]{1,0:T(8,128)S(1)}, u32[]{:S(2)}, u32[]{:S(2)}) %collective-permute-start.12) | collective-permute-done | bytes 98336 | tf_op jit(solution)/shard_map/ppermute | solution.py:197
  72.7 1.3 %collective-permute-done.13 = f32[384,128]{1,0:T(8,128)S(1)} collective-permute-done((f32[384,128]{1,0:T(8,128)S(1)}, f32[384,128]{1,0:T(8,128)S(1)}, u32[]{:S(2)}, u32[]{:S(2)}) %collective-permute-start.13) | collective-permute-done | bytes 196640 | tf_op jit(solution)/shard_map/ppermute | solution.py:201
  74.0 2.8 %copy-done.1 = bf16[64,128,384]{2,1,0:T(8,128)(2,1)S(1)} copy-done((bf16[64,128,384]{2,1,0:T(8,128)(2,1)S(1)}, bf16[64,128,384]{2,1,0:T(8,128)(2,1)}, u32[]{:S(2)}) %copy-start.1) | copy-done | bytes 6291480
  76.8 22.0 %components.1 = (f32[1,384]{1,0:T(1,128)S(1)}, f32[384,384]{1,0:T(8,128)}, f32[64,64,128]{2,1,0:T(8,128)}) custom-call(f32[768,128]{1,0:T(8,128)S(1)} %maximum_select_fusion.packed, f32[384,64]{1,0:T(8,128)S(1)} %copy.5.start, bf16[64,128,384]{2,1,0:T(8,128)(2,1)S(1)} %copy-done.1), custom_call_target="tpu_custom_call" | custom-call | flops 1000000000 | bytes 10000000 | tf_op jit(solution)/shard_map/components/pallas_call | solution.py:303
  98.8 0.6 reduce
  (33 shorter events, 1.1 us)
Async XLA Ops:
  1.7 9.8 %collective-permute-start.1 = (bf16[2,128,384]{2,1,0:T(8,128)(2,1)S(1)}, bf16[2,128,384]{2,1,0:T(8,128)(2,1)S(1)}, u32[]{:S(2)}, u32[]{:S(2)}) collective-permute-start(bf16[2,128,384]{2,1,0:T(8,128)(2,1)S(1)} %get-tuple-element.15), channel_id=1, source_target_pairs={{4,0},{8,4},{12,8},{16,12},{20,16},{24,20},{28,24},{5,1},{9,5},{13... | collective-permute-start | bytes 589832 | tf_op jit(solution)/shard_map/ppermute | solution.py:26
  3.0 12.8 %collective-permute-start = (bf16[2,128,384]{2,1,0:T(8,128)(2,1)S(1)}, bf16[2,128,384]{2,1,0:T(8,128)(2,1)S(1)}, u32[]{:S(2)}, u32[]{:S(2)}) collective-permute-start(bf16[2,128,384]{2,1,0:T(8,128)(2,1)S(1)} %get-tuple-element.16), channel_id=1, source_target_pairs={{0,4},{4,8},{8,12},{12,16},{16,20},{20,24},{24,28},{1,5},{5,9},{9,... | collective-permute-start | bytes 589832 | tf_op jit(solution)/shard_map/ppermute | solution.py:25
  16.0 3.4 %collective-permute-start.2 = (bf16[68,2,384]{2,1,0:T(2,128)(2,1)S(1)}, bf16[68,2,384]{2,1,0:T(2,128)(2,1)S(1)}, u32[]{:S(2)}, u32[]{:S(2)}) collective-permute-start(bf16[68,2,384]{2,1,0:T(2,128)(2,1)S(1)} %pad_maximum_fusion.1), channel_id=1, source_target_pairs={{0,1},{1,2},{2,3},{4,5},{5,6},{6,7},{8,9},{9,10},{10,11},{12,13},{... | collective-permute-start | bytes 313352 | tf_op jit(solution)/shard_map/ppermute | solution.py:332
  18.1 4.3 %collective-permute-start.3 = (bf16[68,2,384]{2,1,0:T(2,128)(2,1)S(1)}, bf16[68,2,384]{2,1,0:T(2,128)(2,1)S(1)}, u32[]{:S(2)}, u32[]{:S(2)}) collective-permute-start(bf16[68,2,384]{2,1,0:T(2,128)(2,1)S(1)} %pad_maximum_fusion.2), channel_id=1, source_target_pairs={{1,0},{2,1},{3,2},{5,4},{6,5},{7,6},{9,8},{10,9},{11,10},{13,12},{... | collective-permute-start | bytes 313352 | tf_op jit(solution)/shard_map/ppermute | solution.py:333
  22.5 2.8 %copy-start.2 = (bf16[64,128,384]{2,1,0:T(8,128)(2,1)S(1)}, bf16[64,128,384]{2,1,0:T(8,128)(2,1)}, u32[]{:S(2)}) copy-start(bf16[64,128,384]{2,1,0:T(8,128)(2,1)} %pixels.1) | copy-start | bytes 18874372
  25.3 47.3 %copy-start.3 = (f32[384,64]{0,1:T(8,128)S(1)}, f32[384,64]{0,1:T(8,128)}, u32[]{:S(2)}) copy-start(f32[384,64]{0,1:T(8,128)} %param.3) | copy-start | bytes 294916
  39.1 2.7 %copy-start = (bf16[64,128,384]{2,1,0:T(8,128)(2,1)}, bf16[64,128,384]{2,1,0:T(8,128)(2,1)S(1)}, u32[]{:S(2)}) copy-start(bf16[64,128,384]{2,1,0:T(8,128)(2,1)S(1)} %get-tuple-element.9.smooth_hbm) | copy-start | bytes 18874372
  41.8 4.4 %collective-permute-start.4 = (f32[384,128]{1,0:T(8,128)S(1)}, f32[384,128]{1,0:T(8,128)S(1)}, u32[]{:S(2)}, u32[]{:S(2)}) collective-permute-start(f32[384,128]{1,0:T(8,128)S(1)} %constant_dynamic-slice_fusion), channel_id=1, source_target_pairs={{0,1},{1,0},{2,3},{3,2},{4,5},{5,4},{6,7},{7,6},{8,9},{9,8},{10,11... | collective-permute-start | bytes 589832 | tf_op jit(solution)/shard_map/ppermute | solution.py:186
  46.3 5.9 %collective-permute-start.5 = (f32[192,128]{1,0:T(8,128)S(1)}, f32[192,128]{1,0:T(8,128)S(1)}, u32[]{:S(2)}, u32[]{:S(2)}) collective-permute-start(f32[192,128]{1,0:T(8,128)S(1)} %get-tuple-element.19), channel_id=1, source_target_pairs={{0,4},{1,5},{2,6},{3,7},{4,0},{5,1},{6,2},{7,3},{8,12},{9,13},{10,... | collective-permute-start | bytes 294920 | tf_op jit(solution)/shard_map/ppermute | solution.py:196
  48.8 4.8 %collective-permute-start.9 = (f32[192,128]{1,0:T(8,128)S(1)}, f32[192,128]{1,0:T(8,128)S(1)}, u32[]{:S(2)}, u32[]{:S(2)}) collective-permute-start(f32[192,128]{1,0:T(8,128)S(1)} %get-tuple-element.20), channel_id=1, source_target_pairs={{0,2},{1,3},{2,0},{3,1},{4,6},{5,7},{6,4},{7,5},{8,10},{9,11},{10,... | collective-permute-start | bytes 294920 | tf_op jit(solution)/shard_map/ppermute | solution.py:197
  53.6 4.7 %collective-permute-start.6 = (f32[192,128]{1,0:T(8,128)S(1)}, f32[192,128]{1,0:T(8,128)S(1)}, u32[]{:S(2)}, u32[]{:S(2)}) collective-permute-start(f32[192,128]{1,0:T(8,128)S(1)} %get-tuple-element.17), channel_id=1, source_target_pairs={{0,2},{1,3},{2,0},{3,1},{4,6},{5,7},{6,4},{7,5},{8,10},{9,11},{10,... | collective-permute-start | bytes 294920 | tf_op jit(solution)/shard_map/ppermute | solution.py:196
  54.0 6.0 %collective-permute-start.10 = (f32[192,128]{1,0:T(8,128)S(1)}, f32[192,128]{1,0:T(8,128)S(1)}, u32[]{:S(2)}, u32[]{:S(2)}) collective-permute-start(f32[192,128]{1,0:T(8,128)S(1)} %get-tuple-element.18), channel_id=1, source_target_pairs={{0,4},{1,5},{2,6},{3,7},{4,0},{5,1},{6,2},{7,3},{8,12},{9,13},{10,... | collective-permute-start | bytes 294920 | tf_op jit(solution)/shard_map/ppermute | solution.py:197
  58.3 5.0 %collective-permute-start.7 = (f32[192,128]{1,0:T(8,128)S(1)}, f32[192,128]{1,0:T(8,128)S(1)}, u32[]{:S(2)}, u32[]{:S(2)}) collective-permute-start(f32[192,128]{1,0:T(8,128)S(1)} %add.257), channel_id=1, source_target_pairs={{0,8},{1,9},{2,10},{3,11},{4,12},{5,13},{6,14},{7,15},{8,0},{9,1},... | collective-permute-start | bytes 294920 | tf_op jit(solution)/shard_map/ppermute | solution.py:196
  60.0 7.7 %collective-permute-start.11 = (f32[192,128]{1,0:T(8,128)S(1)}, f32[192,128]{1,0:T(8,128)S(1)}, u32[]{:S(2)}, u32[]{:S(2)}) collective-permute-start(f32[192,128]{1,0:T(8,128)S(1)} %add.261), channel_id=1, source_target_pairs={{0,16},{1,17},{2,18},{3,19},{4,20},{5,21},{6,22},{7,23},{8,24},{9,... | collective-permute-start | bytes 294920 | tf_op jit(solution)/shard_map/ppermute | solution.py:197
  63.3 6.6 %collective-permute-start.8 = (f32[192,128]{1,0:T(8,128)S(1)}, f32[192,128]{1,0:T(8,128)S(1)}, u32[]{:S(2)}, u32[]{:S(2)}) collective-permute-start(f32[192,128]{1,0:T(8,128)S(1)} %add.258), channel_id=1, source_target_pairs={{0,16},{1,17},{2,18},{3,19},{4,20},{5,21},{6,22},{7,23},{8,24},{9,... | collective-permute-start | bytes 294920 | tf_op jit(solution)/shard_map/ppermute | solution.py:196
  67.7 4.7 %collective-permute-start.12 = (f32[192,128]{1,0:T(8,128)S(1)}, f32[192,128]{1,0:T(8,128)S(1)}, u32[]{:S(2)}, u32[]{:S(2)}) collective-permute-start(f32[192,128]{1,0:T(8,128)S(1)} %add.262), channel_id=1, source_target_pairs={{0,8},{1,9},{2,10},{3,11},{4,12},{5,13},{6,14},{7,15},{8,0},{9,1},... | collective-permute-start | bytes 294920 | tf_op jit(solution)/shard_map/ppermute | solution.py:197
  72.5 1.5 %collective-permute-start.13 = (f32[384,128]{1,0:T(8,128)S(1)}, f32[384,128]{1,0:T(8,128)S(1)}, u32[]{:S(2)}, u32[]{:S(2)}) collective-permute-start(f32[384,128]{1,0:T(8,128)S(1)} %pad_maximum_fusion), channel_id=1, source_target_pairs={{0,1},{1,0},{2,3},{3,2},{4,5},{5,4},{6,7},{7,6},{8,9},{9,8},{10,11... | collective-permute-start | bytes 589832 | tf_op jit(solution)/shard_map/ppermute | solution.py:201
  74.0 2.8 %copy-start.1 = (bf16[64,128,384]{2,1,0:T(8,128)(2,1)S(1)}, bf16[64,128,384]{2,1,0:T(8,128)(2,1)}, u32[]{:S(2)}) copy-start(bf16[64,128,384]{2,1,0:T(8,128)(2,1)} %copy-done) | copy-start | bytes 18874372

commit v3 on v2

--- a/solution.py
+++ b/solution.py
@@ -9,7 +9,7 @@
 
 ITERS = 4
 LANES = 128
-HIGHEST = lax.Precision.HIGHEST
+AHEAD = 16
 
 GAUSS = (0.0625, 0.25, 0.375, 0.25, 0.0625)
 
@@ -144,7 +144,7 @@
     tile_rows, tile_cols, feat = pixels.shape
     n = feat // LANES
     vmem = pl.BlockSpec(memory_space=pltpu.VMEM)
-    hbm = pl.BlockSpec(memory_space=pl.ANY)
+    hbm = pl.BlockSpec(memory_space=pltpu.HBM)
     smem = pl.BlockSpec(memory_space=pltpu.SMEM)
     return pl.pallas_call(
         smooth_kernel,
@@ -209,35 +209,65 @@
     work = jnp.concatenate([a, (row == col).astype(jnp.float32)], axis=1)
     blocks = [work[8 * i : 8 * i + 8] for i in range(n // 8)]
     sub = lax.broadcasted_iota(jnp.int32, (8, 2 * n), 0)
-    ahead = 4
+    ahead = min(AHEAD, n)
     pivots = []
     for j0 in range(0, n, ahead):
         first = j0 // 8
-        cols = [[jnp.broadcast_to(b[:, j0 + k : j0 + k + 1], (8, 2 * n)) for b in blocks[first:]] for k in range(ahead)]
+        cols = [
+            {i: jnp.broadcast_to(blocks[i][:, j : j + 1], (8, 2 * n)) for i in range(j // 8, n // 8)}
+            for j in range(j0, j0 + ahead)
+        ]
         for k in range(ahead):
             j = j0 + k
-            s = j - 8 * first
-            recip = 1.0 / jnp.broadcast_to(cols[k][0][s : s + 1], (8, 2 * n))
+            top = j // 8
+            s = j - 8 * top
+            recip = 1.0 / jnp.broadcast_to(cols[k][top][s : s + 1], (8, 2 * n))
             pivots.append(recip)
-            line = jnp.broadcast_to(blocks[first][s : s + 1], (8, 2 * n)) * recip
-            factor = [c for c in cols[k]]
-            factor[0] = jnp.where(sub > s, factor[0], 0.0)
-            later = [jnp.broadcast_to(cols[m][0][s : s + 1], (8, 2 * n)) * recip for m in range(k + 1, ahead)]
-            for i in range(first, n // 8):
-                for m in range(k + 1, ahead):
-                    cols[m][i - first] = cols[m][i - first] - factor[i - first] * later[m - k - 1]
-                blocks[i] = blocks[i] - factor[i - first] * line
+            factor = dict(cols[k])
+            factor[top] = jnp.where(sub > s, factor[top], 0.0)
+            for m in range(k + 1, ahead):
+                other = (j0 + m) // 8
+                t = j0 + m - 8 * other
+                scaled = jnp.broadcast_to(cols[k][other][t : t + 1], (8, 2 * n)) * recip
+                for i in cols[m]:
+                    cols[m][i] = cols[m][i] - factor[i] * scaled
+            line = jnp.broadcast_to(blocks[top][s : s + 1], (8, 2 * n)) * recip
+            for i in range(top, n // 8):
+                blocks[i] = blocks[i] - factor[i] * line
     out = []
     for i in range(n // 8):
-        scale = jnp.zeros((8, 2 * n), jnp.float32)
-        for s in range(8):
+        scale = pivots[8 * i]
+        for s in range(1, 8):
             scale = jnp.where(sub == s, pivots[8 * i + s], scale)
-        out.append((blocks[i] * lax.rsqrt(1.0 / scale))[:, n:])
+        out.append((blocks[i] * lax.sqrt(scale))[:, n:])
     return jnp.concatenate(out, axis=0)
 
 
-def dot(a, b, contract, precision=HIGHEST):
-    return lax.dot_general(a, b, (contract, ((), ())), precision=precision, preferred_element_type=jnp.float32)
+def thirds(x):
+    high = x.astype(jnp.bfloat16)
+    rest = x - high.astype(jnp.float32)
+    middle = rest.astype(jnp.bfloat16)
+    return high, middle, (rest - middle.astype(jnp.float32)).astype(jnp.bfloat16)
+
+
+def dot(a, b, contract):
+    return lax.dot_general(a, b, (contract, ((), ())), preferred_element_type=jnp.float32)
+
+
+def dot_thirds(a, b):
+    m = a[0].shape[0]
+    one = dot(jnp.concatenate(a, axis=0), b[0], ((1,), (0,)))
+    two = dot(jnp.concatenate(a[:2], axis=0), b[1], ((1,), (0,)))
+    low = one[2 * m :] + two[m:] + dot(a[0], b[2], ((1,), (0,)))
+    return one[:m] + (one[m : 2 * m] + two[:m] + low)
+
+
+def gram_thirds(y):
+    m = y[0].shape[0]
+    stack = jnp.concatenate(y, axis=0)
+    p = dot(stack, stack, ((1,), (1,)))
+    part = lambda i, j: p[i * m : (i + 1) * m, j * m : (j + 1) * m]
+    return part(0, 0) + ((part(0, 1) + part(1, 0)) + (part(1, 1) + (part(0, 2) + part(2, 0))))
 
 
 def components_kernel(count, packed, start, smooth_hbm, mean_out, proj_out, scores_hbm, cov, smooth, scores, in_sem, out_sem):
@@ -274,12 +304,18 @@
             cov[i * LANES : (i + 1) * LANES, j * LANES : (j + 1) * LANES] = c
             if i != j:
                 cov[j * LANES : (j + 1) * LANES, i * LANES : (i + 1) * LANES] = c.T
-    basis = start[...].T
+    cov_thirds = thirds(cov[...])
+    y = dot_thirds(thirds(start[...].T), cov_thirds)
     for step in range(ITERS):
-        y = dot(basis, cov[...], ((1,), (0,)))
-        lower = inverse_factor(dot(y, y, ((1,), (1,))))
-        basis = dot(lower, y, ((1,), (0,)))
-    proj_out[...] = dot(basis, basis, ((0,), (0,)))
+        parts = thirds(y)
+        z = y if step == ITERS - 1 else dot_thirds(parts, cov_thirds)
+        lower = inverse_factor(gram_thirds(parts))
+        y = dot_thirds(thirds(lower), thirds(z))
+    basis = y
+    b = thirds(basis)
+    left = jnp.concatenate([b[0], b[0], b[1], b[1], b[0], b[2]], axis=0)
+    right = jnp.concatenate([b[0], b[1], b[0], b[1], b[2], b[0]], axis=0)
+    proj_out[...] = dot(left, right, ((0,), (0,)))
     basis_b = basis.astype(jnp.bfloat16)
     shift = jnp.sum(basis_b.astype(jnp.float32) * mean, axis=1, keepdims=True)
     shift = jnp.broadcast_to(shift, (rank, LANES))
@@ -299,7 +335,7 @@
     tile_rows, tile_cols, feat = smoothed.shape
     rank = start.shape[1]
     vmem = pl.BlockSpec(memory_space=pltpu.VMEM)
-    hbm = pl.BlockSpec(memory_space=pl.ANY)
+    hbm = pl.BlockSpec(memory_space=pltpu.HBM)
     return pl.pallas_call(
         functools.partial(components_kernel, count),
         out_shape=(

time: 99.7 us -> 94 us (0.943)
  Pallas kernels: 35.8 us -> 30.1 us
    pallas_call x1, Pallas kernels: 22 us -> 16.3 us  [components(): pl.pallas_call(functools.partial(components_kernel, count), out_shape=(ja...]
where the time goes in v3:
time: 94 us; the launch traced here: 93.7 us
  Pallas kernels  30.1 us (32%)
  waiting for transfers between devices  27.4 us (29%)
  starting transfers between devices  23.3 us (25%)
  local copies, waits for them, and re-layouts  10.8 us (11%)
  other arithmetic  1.24 us (1%)
    pallas_call x1, Pallas kernels, components(): pl.pallas_call(functools.partial(components_kernel, count), out_shape=(ja...  16.3 us
    pallas_call x1, Pallas kernels, smooth_and_gram(): pl.pallas_call(smooth_kernel, out_shape=(jax.ShapeDtypeStruct(pixels.shap...  13.8 us
    ppermute x4, waiting for transfers between devices, all_sum(): got_a = lax.ppermute(a, axes, first)  10.8 us
    unnamed x9, local copies, waits for them, and re-layouts  8.34 us
    ppermute x4, starting transfers between devices, all_sum(): got_a = lax.ppermute(a, axes, first)  7.4 us
    ppermute x1, starting transfers between devices, edges_2(): lax.ppermute(lax.slice_in_dim(shard, length - WIDTH, length, axis=dim), a...  5.51 us
    ppermute x4, waiting for transfers between devices, all_sum(): got_b = lax.ppermute(b, axes, second)  5.46 us
    ppermute x1, waiting for transfers between devices, edges_2(): lax.ppermute(lax.slice_in_dim(shard, length - WIDTH, length, axis=dim), a...  4.35 us
  transfers between devices with their start and end apart: 14, of which 12 were waited for; matrix products, arithmetic and copies ran while one was open for 2% of the time, Pallas kernels for 0%

profile of v3, /device:TPU:0, one launch (start us, length us, event | category | flops | bytes accessed | tf_op | source)
XLA Modules:
  0.0 93.7 jit_solution(9298812835314965741)
XLA Ops:
  0.6 1.1 %fusion.11 = (bf16[2,128,384]{2,1,0:T(8,128)(2,1)S(1)}, bf16[2,128,384]{2,1,0:T(8,128)(2,1)S(1)}) fusion(bf16[64,128,384]{2,1,0:T(8,128)(2,1)} %pixels.1), kind=kLoop, calls=%fused_computation.41 | loop fusion | bytes 786432 | tf_op jit(solution)/shard_map/slice | solution.py:26
  1.7 1.3 %collective-permute-start.1 = (bf16[2,128,384]{2,1,0:T(8,128)(2,1)S(1)}, bf16[2,128,384]{2,1,0:T(8,128)(2,1)S(1)}, u32[]{:S(2)}, u32[]{:S(2)}) collective-permute-start(bf16[2,128,384]{2,1,0:T(8,128)(2,1)S(1)} %get-tuple-element.15), channel_id=1, source_target_pairs={{4,0},{8,4},{12,8},{16,12},{20,16},{24,20},{28,24},{5,1},{9,5},{13... | collective-permute-start | bytes 589832 | tf_op jit(solution)/shard_map/ppermute | solution.py:26
  3.0 5.5 %collective-permute-start = (bf16[2,128,384]{2,1,0:T(8,128)(2,1)S(1)}, bf16[2,128,384]{2,1,0:T(8,128)(2,1)S(1)}, u32[]{:S(2)}, u32[]{:S(2)}) collective-permute-start(bf16[2,128,384]{2,1,0:T(8,128)(2,1)S(1)} %get-tuple-element.16), channel_id=1, source_target_pairs={{0,4},{4,8},{8,12},{12,16},{16,20},{20,24},{24,28},{1,5},{5,9},{9,... | collective-permute-start | bytes 589832 | tf_op jit(solution)/shard_map/ppermute | solution.py:25
  8.6 1.3 %fusion.10 = (bf16[64,2,384]{2,1,0:T(2,128)(2,1)S(1)}, bf16[64,2,384]{2,1,0:T(2,128)(2,1)S(1)}) fusion(bf16[64,128,384]{2,1,0:T(8,128)(2,1)} %pixels.1), kind=kLoop, calls=%fused_computation.40 | loop fusion | bytes 393216 | tf_op jit(solution)/shard_map/slice | solution.py:366
  10.0 1.4 %collective-permute-done.1.below = bf16[2,128,384]{2,1,0:T(8,128)(2,1)S(1)} collective-permute-done((bf16[2,128,384]{2,1,0:T(8,128)(2,1)S(1)}, bf16[2,128,384]{2,1,0:T(8,128)(2,1)S(1)}, u32[]{:S(2)}, u32[]{:S(2)}) %collective-permute-start.1) | collective-permute-done | bytes 196640 | tf_op jit(solution)/shard_map/ppermute | solution.py:26
  11.5 4.4 %collective-permute-done.above = bf16[2,128,384]{2,1,0:T(8,128)(2,1)S(1)} collective-permute-done((bf16[2,128,384]{2,1,0:T(8,128)(2,1)S(1)}, bf16[2,128,384]{2,1,0:T(8,128)(2,1)S(1)}, u32[]{:S(2)}, u32[]{:S(2)}) %collective-permute-start) | collective-permute-done | bytes 196640 | tf_op jit(solution)/shard_map/ppermute | solution.py:25
  16.0 1.9 %collective-permute-start.2 = (bf16[68,2,384]{2,1,0:T(2,128)(2,1)S(1)}, bf16[68,2,384]{2,1,0:T(2,128)(2,1)S(1)}, u32[]{:S(2)}, u32[]{:S(2)}) collective-permute-start(bf16[68,2,384]{2,1,0:T(2,128)(2,1)S(1)} %pad_maximum_fusion.1), channel_id=1, source_target_pairs={{0,1},{1,2},{2,3},{4,5},{5,6},{6,7},{8,9},{9,10},{10,11},{12,13},{... | collective-permute-start | bytes 313352 | tf_op jit(solution)/shard_map/ppermute | solution.py:368
  18.1 1.3 %collective-permute-start.3 = (bf16[68,2,384]{2,1,0:T(2,128)(2,1)S(1)}, bf16[68,2,384]{2,1,0:T(2,128)(2,1)S(1)}, u32[]{:S(2)}, u32[]{:S(2)}) collective-permute-start(bf16[68,2,384]{2,1,0:T(2,128)(2,1)S(1)} %pad_maximum_fusion.2), channel_id=1, source_target_pairs={{1,0},{2,1},{3,2},{5,4},{6,5},{7,6},{9,8},{10,9},{11,10},{13,12},{... | collective-permute-start | bytes 313352 | tf_op jit(solution)/shard_map/ppermute | solution.py:369
  19.4 3.0 %collective-permute-done.3.right = bf16[68,2,384]{2,1,0:T(2,128)(2,1)S(1)} collective-permute-done((bf16[68,2,384]{2,1,0:T(2,128)(2,1)S(1)}, bf16[68,2,384]{2,1,0:T(2,128)(2,1)S(1)}, u32[]{:S(2)}, u32[]{:S(2)}) %collective-permute-start.3) | collective-permute-done | bytes 104480 | tf_op jit(solution)/shard_map/ppermute | solution.py:369
  22.5 2.8 %copy-done.2 = bf16[64,128,384]{2,1,0:T(8,128)(2,1)S(1)} copy-done((bf16[64,128,384]{2,1,0:T(8,128)(2,1)S(1)}, bf16[64,128,384]{2,1,0:T(8,128)(2,1)}, u32[]{:S(2)}) %copy-start.2) | copy-done | bytes 6291480
  25.3 13.8 %smooth.1 = (bf16[64,128,384]{2,1,0:T(8,128)(2,1)S(1)}, f32[768,128]{1,0:T(8,128)S(1)}) custom-call(f32[64]{0:T(128)S(1)} %fusion.9.row_scale, bf16[64,128,384]{2,1,0:T(8,128)(2,1)S(1)} %copy-done.2, bf16[2,128,384]{2,1,0:T(8,128)(2,1)S(1)} %collective-permute-done.above, bf16[2,128,384]{2,1,0:T(8,128)(2,1)S(1)} %collective-permute-done.1.below, ...), custom_call_target="tpu_custom_call" | custom-call | flops 5000000000 | bytes 20000000 | tf_op jit(solution)/shard_map/smooth/pallas_call | solution.py:149
  39.1 2.6 %copy-done = bf16[64,128,384]{2,1,0:T(8,128)(2,1)} copy-done((bf16[64,128,384]{2,1,0:T(8,128)(2,1)}, bf16[64,128,384]{2,1,0:T(8,128)(2,1)S(1)}, u32[]{:S(2)}) %copy-start) | copy-done | bytes 6291480
  41.8 3.4 %collective-permute-start.4 = (f32[384,128]{1,0:T(8,128)S(1)}, f32[384,128]{1,0:T(8,128)S(1)}, u32[]{:S(2)}, u32[]{:S(2)}) collective-permute-start(f32[384,128]{1,0:T(8,128)S(1)} %constant_dynamic-slice_fusion), channel_id=1, source_target_pairs={{0,1},{1,0},{2,3},{3,2},{4,5},{5,4},{6,7},{7,6},{8,9},{9,8},{10,11... | collective-permute-start | bytes 589832 | tf_op jit(solution)/shard_map/ppermute | solution.py:186
  45.1 1.1 %collective-permute-done.4 = f32[384,128]{1,0:T(8,128)S(1)} collective-permute-done((f32[384,128]{1,0:T(8,128)S(1)}, f32[384,128]{1,0:T(8,128)S(1)}, u32[]{:S(2)}, u32[]{:S(2)}) %collective-permute-start.4) | collective-permute-done | bytes 196640 | tf_op jit(solution)/shard_map/ppermute | solution.py:186
  46.3 2.5 %collective-permute-start.5 = (f32[192,128]{1,0:T(8,128)S(1)}, f32[192,128]{1,0:T(8,128)S(1)}, u32[]{:S(2)}, u32[]{:S(2)}) collective-permute-start(f32[192,128]{1,0:T(8,128)S(1)} %get-tuple-element.19), channel_id=1, source_target_pairs={{0,4},{1,5},{2,6},{3,7},{4,0},{5,1},{6,2},{7,3},{8,12},{9,13},{10,... | collective-permute-start | bytes 294920 | tf_op jit(solution)/shard_map/ppermute | solution.py:196
  49.0 3.2 %collective-permute-done.5 = f32[192,128]{1,0:T(8,128)S(1)} collective-permute-done((f32[192,128]{1,0:T(8,128)S(1)}, f32[192,128]{1,0:T(8,128)S(1)}, u32[]{:S(2)}, u32[]{:S(2)}) %collective-permute-start.5) | collective-permute-done | bytes 98336 | tf_op jit(solution)/shard_map/ppermute | solution.py:196
  52.1 1.5 %collective-permute-done.9 = f32[192,128]{1,0:T(8,128)S(1)} collective-permute-done((f32[192,128]{1,0:T(8,128)S(1)}, f32[192,128]{1,0:T(8,128)S(1)}, u32[]{:S(2)}, u32[]{:S(2)}) %collective-permute-start.9) | collective-permute-done | bytes 98336 | tf_op jit(solution)/shard_map/ppermute | solution.py:197
  53.6 0.3 collective-permute-start.6
  54.0 0.4 collective-permute-start.10
  54.3 4.0 %collective-permute-done.6 = f32[192,128]{1,0:T(8,128)S(1)} collective-permute-done((f32[192,128]{1,0:T(8,128)S(1)}, f32[192,128]{1,0:T(8,128)S(1)}, u32[]{:S(2)}, u32[]{:S(2)}) %collective-permute-start.6) | collective-permute-done | bytes 98336 | tf_op jit(solution)/shard_map/ppermute | solution.py:196
  58.3 1.6 %collective-permute-start.7 = (f32[192,128]{1,0:T(8,128)S(1)}, f32[192,128]{1,0:T(8,128)S(1)}, u32[]{:S(2)}, u32[]{:S(2)}) collective-permute-start(f32[192,128]{1,0:T(8,128)S(1)} %add.257), channel_id=1, source_target_pairs={{0,8},{1,9},{2,10},{3,11},{4,12},{5,13},{6,14},{7,15},{8,0},{9,1},... | collective-permute-start | bytes 294920 | tf_op jit(solution)/shard_map/ppermute | solution.py:196
  60.0 1.3 %collective-permute-start.11 = (f32[192,128]{1,0:T(8,128)S(1)}, f32[192,128]{1,0:T(8,128)S(1)}, u32[]{:S(2)}, u32[]{:S(2)}) collective-permute-start(f32[192,128]{1,0:T(8,128)S(1)} %add.261), channel_id=1, source_target_pairs={{0,16},{1,17},{2,18},{3,19},{4,20},{5,21},{6,22},{7,23},{8,24},{9,... | collective-permute-start | bytes 294920 | tf_op jit(solution)/shard_map/ppermute | solution.py:197
  61.3 2.0 %collective-permute-done.7 = f32[192,128]{1,0:T(8,128)S(1)} collective-permute-done((f32[192,128]{1,0:T(8,128)S(1)}, f32[192,128]{1,0:T(8,128)S(1)}, u32[]{:S(2)}, u32[]{:S(2)}) %collective-permute-start.7) | collective-permute-done | bytes 98336 | tf_op jit(solution)/shard_map/ppermute | solution.py:196
  63.3 2.9 %collective-permute-start.8 = (f32[192,128]{1,0:T(8,128)S(1)}, f32[192,128]{1,0:T(8,128)S(1)}, u32[]{:S(2)}, u32[]{:S(2)}) collective-permute-start(f32[192,128]{1,0:T(8,128)S(1)} %add.258), channel_id=1, source_target_pairs={{0,16},{1,17},{2,18},{3,19},{4,20},{5,21},{6,22},{7,23},{8,24},{9,... | collective-permute-start | bytes 294920 | tf_op jit(solution)/shard_map/ppermute | solution.py:196
  66.2 1.5 %collective-permute-done.11 = f32[192,128]{1,0:T(8,128)S(1)} collective-permute-done((f32[192,128]{1,0:T(8,128)S(1)}, f32[192,128]{1,0:T(8,128)S(1)}, u32[]{:S(2)}, u32[]{:S(2)}) %collective-permute-start.11) | collective-permute-done | bytes 98336 | tf_op jit(solution)/shard_map/ppermute | solution.py:197
  67.7 0.6 collective-permute-start.12
  68.3 1.6 %collective-permute-done.8 = f32[192,128]{1,0:T(8,128)S(1)} collective-permute-done((f32[192,128]{1,0:T(8,128)S(1)}, f32[192,128]{1,0:T(8,128)S(1)}, u32[]{:S(2)}, u32[]{:S(2)}) %collective-permute-start.8) | collective-permute-done | bytes 98336 | tf_op jit(solution)/shard_map/ppermute | solution.py:196
  70.0 2.5 %collective-permute-done.12 = f32[192,128]{1,0:T(8,128)S(1)} collective-permute-done((f32[192,128]{1,0:T(8,128)S(1)}, f32[192,128]{1,0:T(8,128)S(1)}, u32[]{:S(2)}, u32[]{:S(2)}) %collective-permute-start.12) | collective-permute-done | bytes 98336 | tf_op jit(solution)/shard_map/ppermute | solution.py:197
  72.7 1.3 %collective-permute-done.13 = f32[384,128]{1,0:T(8,128)S(1)} collective-permute-done((f32[384,128]{1,0:T(8,128)S(1)}, f32[384,128]{1,0:T(8,128)S(1)}, u32[]{:S(2)}, u32[]{:S(2)}) %collective-permute-start.13) | collective-permute-done | bytes 196640 | tf_op jit(solution)/shard_map/ppermute | solution.py:201
  74.0 2.8 %copy-done.1 = bf16[64,128,384]{2,1,0:T(8,128)(2,1)S(1)} copy-done((bf16[64,128,384]{2,1,0:T(8,128)(2,1)S(1)}, bf16[64,128,384]{2,1,0:T(8,128)(2,1)}, u32[]{:S(2)}) %copy-start.1) | copy-done | bytes 6291480
  76.8 16.3 %components.1 = (f32[1,384]{1,0:T(1,128)S(1)}, f32[384,384]{1,0:T(8,128)}, f32[64,64,128]{2,1,0:T(8,128)}) custom-call(f32[768,128]{1,0:T(8,128)S(1)} %maximum_select_fusion.packed, f32[384,64]{1,0:T(8,128)S(1)} %copy.5.start, bf16[64,128,384]{2,1,0:T(8,128)(2,1)S(1)} %copy-done.1), custom_call_target="tpu_custom_call" | custom-call | flops 1000000000 | bytes 10000000 | tf_op jit(solution)/shard_map/components/pallas_call | solution.py:339
  93.1 0.6 reduce
  (33 shorter events, 1.1 us)
Async XLA Ops:
  1.7 9.8 %collective-permute-start.1 = (bf16[2,128,384]{2,1,0:T(8,128)(2,1)S(1)}, bf16[2,128,384]{2,1,0:T(8,128)(2,1)S(1)}, u32[]{:S(2)}, u32[]{:S(2)}) collective-permute-start(bf16[2,128,384]{2,1,0:T(8,128)(2,1)S(1)} %get-tuple-element.15), channel_id=1, source_target_pairs={{4,0},{8,4},{12,8},{16,12},{20,16},{24,20},{28,24},{5,1},{9,5},{13... | collective-permute-start | bytes 589832 | tf_op jit(solution)/shard_map/ppermute | solution.py:26
  3.0 12.8 %collective-permute-start = (bf16[2,128,384]{2,1,0:T(8,128)(2,1)S(1)}, bf16[2,128,384]{2,1,0:T(8,128)(2,1)S(1)}, u32[]{:S(2)}, u32[]{:S(2)}) collective-permute-start(bf16[2,128,384]{2,1,0:T(8,128)(2,1)S(1)} %get-tuple-element.16), channel_id=1, source_target_pairs={{0,4},{4,8},{8,12},{12,16},{16,20},{20,24},{24,28},{1,5},{5,9},{9,... | collective-permute-start | bytes 589832 | tf_op jit(solution)/shard_map/ppermute | solution.py:25
  16.0 3.4 %collective-permute-start.2 = (bf16[68,2,384]{2,1,0:T(2,128)(2,1)S(1)}, bf16[68,2,384]{2,1,0:T(2,128)(2,1)S(1)}, u32[]{:S(2)}, u32[]{:S(2)}) collective-permute-start(bf16[68,2,384]{2,1,0:T(2,128)(2,1)S(1)} %pad_maximum_fusion.1), channel_id=1, source_target_pairs={{0,1},{1,2},{2,3},{4,5},{5,6},{6,7},{8,9},{9,10},{10,11},{12,13},{... | collective-permute-start | bytes 313352 | tf_op jit(solution)/shard_map/ppermute | solution.py:368
  18.1 4.3 %collective-permute-start.3 = (bf16[68,2,384]{2,1,0:T(2,128)(2,1)S(1)}, bf16[68,2,384]{2,1,0:T(2,128)(2,1)S(1)}, u32[]{:S(2)}, u32[]{:S(2)}) collective-permute-start(bf16[68,2,384]{2,1,0:T(2,128)(2,1)S(1)} %pad_maximum_fusion.2), channel_id=1, source_target_pairs={{1,0},{2,1},{3,2},{5,4},{6,5},{7,6},{9,8},{10,9},{11,10},{13,12},{... | collective-permute-start | bytes 313352 | tf_op jit(solution)/shard_map/ppermute | solution.py:369
  22.5 2.8 %copy-start.2 = (bf16[64,128,384]{2,1,0:T(8,128)(2,1)S(1)}, bf16[64,128,384]{2,1,0:T(8,128)(2,1)}, u32[]{:S(2)}) copy-start(bf16[64,128,384]{2,1,0:T(8,128)(2,1)} %pixels.1) | copy-start | bytes 18874372
  25.3 47.3 %copy-start.3 = (f32[384,64]{0,1:T(8,128)S(1)}, f32[384,64]{0,1:T(8,128)}, u32[]{:S(2)}) copy-start(f32[384,64]{0,1:T(8,128)} %param.3) | copy-start | bytes 294916
  39.1 2.7 %copy-start = (bf16[64,128,384]{2,1,0:T(8,128)(2,1)}, bf16[64,128,384]{2,1,0:T(8,128)(2,1)S(1)}, u32[]{:S(2)}) copy-start(bf16[64,128,384]{2,1,0:T(8,128)(2,1)S(1)} %get-tuple-element.9.smooth_hbm) | copy-start | bytes 18874372
  41.8 4.4 %collective-permute-start.4 = (f32[384,128]{1,0:T(8,128)S(1)}, f32[384,128]{1,0:T(8,128)S(1)}, u32[]{:S(2)}, u32[]{:S(2)}) collective-permute-start(f32[384,128]{1,0:T(8,128)S(1)} %constant_dynamic-slice_fusion), channel_id=1, source_target_pairs={{0,1},{1,0},{2,3},{3,2},{4,5},{5,4},{6,7},{7,6},{8,9},{9,8},{10,11... | collective-permute-start | bytes 589832 | tf_op jit(solution)/shard_map/ppermute | solution.py:186
  46.3 5.9 %collective-permute-start.5 = (f32[192,128]{1,0:T(8,128)S(1)}, f32[192,128]{1,0:T(8,128)S(1)}, u32[]{:S(2)}, u32[]{:S(2)}) collective-permute-start(f32[192,128]{1,0:T(8,128)S(1)} %get-tuple-element.19), channel_id=1, source_target_pairs={{0,4},{1,5},{2,6},{3,7},{4,0},{5,1},{6,2},{7,3},{8,12},{9,13},{10,... | collective-permute-start | bytes 294920 | tf_op jit(solution)/shard_map/ppermute | solution.py:196
  48.8 4.8 %collective-permute-start.9 = (f32[192,128]{1,0:T(8,128)S(1)}, f32[192,128]{1,0:T(8,128)S(1)}, u32[]{:S(2)}, u32[]{:S(2)}) collective-permute-start(f32[192,128]{1,0:T(8,128)S(1)} %get-tuple-element.20), channel_id=1, source_target_pairs={{0,2},{1,3},{2,0},{3,1},{4,6},{5,7},{6,4},{7,5},{8,10},{9,11},{10,... | collective-permute-start | bytes 294920 | tf_op jit(solution)/shard_map/ppermute | solution.py:197
  53.6 4.7 %collective-permute-start.6 = (f32[192,128]{1,0:T(8,128)S(1)}, f32[192,128]{1,0:T(8,128)S(1)}, u32[]{:S(2)}, u32[]{:S(2)}) collective-permute-start(f32[192,128]{1,0:T(8,128)S(1)} %get-tuple-element.17), channel_id=1, source_target_pairs={{0,2},{1,3},{2,0},{3,1},{4,6},{5,7},{6,4},{7,5},{8,10},{9,11},{10,... | collective-permute-start | bytes 294920 | tf_op jit(solution)/shard_map/ppermute | solution.py:196
  54.0 6.0 %collective-permute-start.10 = (f32[192,128]{1,0:T(8,128)S(1)}, f32[192,128]{1,0:T(8,128)S(1)}, u32[]{:S(2)}, u32[]{:S(2)}) collective-permute-start(f32[192,128]{1,0:T(8,128)S(1)} %get-tuple-element.18), channel_id=1, source_target_pairs={{0,4},{1,5},{2,6},{3,7},{4,0},{5,1},{6,2},{7,3},{8,12},{9,13},{10,... | collective-permute-start | bytes 294920 | tf_op jit(solution)/shard_map/ppermute | solution.py:197
  58.3 5.0 %collective-permute-start.7 = (f32[192,128]{1,0:T(8,128)S(1)}, f32[192,128]{1,0:T(8,128)S(1)}, u32[]{:S(2)}, u32[]{:S(2)}) collective-permute-start(f32[192,128]{1,0:T(8,128)S(1)} %add.257), channel_id=1, source_target_pairs={{0,8},{1,9},{2,10},{3,11},{4,12},{5,13},{6,14},{7,15},{8,0},{9,1},... | collective-permute-start | bytes 294920 | tf_op jit(solution)/shard_map/ppermute | solution.py:196
  60.0 7.7 %collective-permute-start.11 = (f32[192,128]{1,0:T(8,128)S(1)}, f32[192,128]{1,0:T(8,128)S(1)}, u32[]{:S(2)}, u32[]{:S(2)}) collective-permute-start(f32[192,128]{1,0:T(8,128)S(1)} %add.261), channel_id=1, source_target_pairs={{0,16},{1,17},{2,18},{3,19},{4,20},{5,21},{6,22},{7,23},{8,24},{9,... | collective-permute-start | bytes 294920 | tf_op jit(solution)/shard_map/ppermute | solution.py:197
  63.3 6.6 %collective-permute-start.8 = (f32[192,128]{1,0:T(8,128)S(1)}, f32[192,128]{1,0:T(8,128)S(1)}, u32[]{:S(2)}, u32[]{:S(2)}) collective-permute-start(f32[192,128]{1,0:T(8,128)S(1)} %add.258), channel_id=1, source_target_pairs={{0,16},{1,17},{2,18},{3,19},{4,20},{5,21},{6,22},{7,23},{8,24},{9,... | collective-permute-start | bytes 294920 | tf_op jit(solution)/shard_map/ppermute | solution.py:196
  67.7 4.7 %collective-permute-start.12 = (f32[192,128]{1,0:T(8,128)S(1)}, f32[192,128]{1,0:T(8,128)S(1)}, u32[]{:S(2)}, u32[]{:S(2)}) collective-permute-start(f32[192,128]{1,0:T(8,128)S(1)} %add.262), channel_id=1, source_target_pairs={{0,8},{1,9},{2,10},{3,11},{4,12},{5,13},{6,14},{7,15},{8,0},{9,1},... | collective-permute-start | bytes 294920 | tf_op jit(solution)/shard_map/ppermute | solution.py:197
  72.5 1.5 %collective-permute-start.13 = (f32[384,128]{1,0:T(8,128)S(1)}, f32[384,128]{1,0:T(8,128)S(1)}, u32[]{:S(2)}, u32[]{:S(2)}) collective-permute-start(f32[384,128]{1,0:T(8,128)S(1)} %pad_maximum_fusion), channel_id=1, source_target_pairs={{0,1},{1,0},{2,3},{3,2},{4,5},{5,4},{6,7},{7,6},{8,9},{9,8},{10,11... | collective-permute-start | bytes 589832 | tf_op jit(solution)/shard_map/ppermute | solution.py:201
  74.0 2.8 %copy-start.1 = (bf16[64,128,384]{2,1,0:T(8,128)(2,1)S(1)}, bf16[64,128,384]{2,1,0:T(8,128)(2,1)}, u32[]{:S(2)}) copy-start(bf16[64,128,384]{2,1,0:T(8,128)(2,1)} %copy-done) | copy-start | bytes 18874372
